TPU v7x, 512 devices: a whole 4x4x16 slice. The times are simulated.
512 devices in a mesh: rows: 128 (over z, x, core), cols: 4 (over y).
Axes of the slice: x: 4, y: 4, z: 16, core: 2. Of those that a mesh axis runs over, the one named last changes fastest.
Arguments:
- tile_density: bfloat16 [32768, 64, 64], P(('rows', 'cols')), may hold values from -6 to 6
- tile_dest: int32 [32768, 1], P(('rows', 'cols')), may hold values from 0 to 127; in each aligned block of 64 rows (0 to 63, 64 to 127, ...) at most 2 rows name the same one
- tile_place: int32 [32768], P(('rows', 'cols')), may hold values from 0 to 31
- psf_spectrum: bfloat16 [32768, 2048], P('rows', 'cols'), may hold values from 0.049804688 to 1
Outputs:
- flare_spectrum: float32 [32768, 2, 2048], P('rows', None, 'cols')
Inputs may be any that keep to these rules, and one draw needn't show every extreme that they name: `tile_dest`: among the 64 tiles of one owner, at most 2 lie in the same row slab, and some owner has exactly 2 in one row slab.
All inputs are finite; a program needn't handle non-finite values.
Results may differ from a plain program's by a relative error of at most 0.0075.
Values may be sent and summed in bfloat16 or wider, within the bound.
No kernel may reach another device: no remote copies, remote signals or barrier semaphores. Data moves between devices by JAX's collectives and lax.ppermute only.
A program may use at most 64 MiB of HBM per device.

v0:
```python
import math

import jax
import jax.numpy as jnp
from jax import lax
from jax.sharding import PartitionSpec as P


def joined_along(pieces, dim):
    pieces = jnp.moveaxis(pieces, 0, dim)
    lengths = pieces.shape
    return pieces.reshape(*lengths[:dim], lengths[dim] * lengths[dim + 1], *lengths[dim + 2 :])


def sent_to_all(x, axis):
    size = lax.axis_size(axis)
    return lax.all_to_all(jnp.broadcast_to(x[None], (size, *x.shape)), axis, 0, 0, tiled=True)


def gathered_copies(x, axis, dim):
    return joined_along(sent_to_all(x, axis), dim)


def make_table(length, factor):
    positions = jnp.arange(length, dtype=jnp.int32)
    angles = (
        2.0
        * math.pi
        / length
        * (positions[:, None] * positions[None, :] % length).astype(jnp.float32)
    )
    cosine = jnp.cos(angles) * factor
    sine_part = jnp.sin(angles) * factor
    upper_rows = jnp.stack([cosine, -sine_part], 1)
    bottom = jnp.stack([sine_part, cosine], 1)
    return jnp.stack([upper_rows, bottom], 0).astype(jnp.bfloat16)


def twiddle(real_part, imag_part, position, frequency, period):
    angles = 2.0 * math.pi / period * (position * frequency % period).astype(jnp.float32)
    cosine = jnp.cos(angles)
    sine_part = jnp.sin(angles)
    return (real_part * cosine + imag_part * sine_part, imag_part * cosine - real_part * sine_part)


def on_device(tile_density, tile_dest, tile_place, psf_spectrum):
    tile_count, tile_side, _ = tile_density.shape
    rows_dev, cols_dev = psf_spectrum.shape
    rows_n = lax.axis_size("rows")
    cols_n = lax.axis_size("cols")
    capacity = max(2, 2 * tile_count // rows_n)
    slot_total = rows_n * capacity
    target = tile_dest[:, 0]
    matches = (target[:, None] == jnp.arange(rows_n, dtype=jnp.int32)[None, :]).astype(jnp.int32)
    order_within = jnp.sum((jnp.cumsum(matches, 0) - matches) * matches, 1)
    slot_index = target * capacity + order_within
    chosen = slot_index[:, None] == jnp.arange(slot_total, dtype=jnp.int32)[None, :]
    tiles_flat = tile_density.reshape(tile_count, tile_side * tile_side)
    outgoing = jnp.einsum(
        "ts,tc->sc", chosen.astype(jnp.bfloat16), tiles_flat, preferred_element_type=jnp.float32
    ).astype(jnp.bfloat16)
    labels = jnp.sum(jnp.where(chosen, (tile_place + 1)[:, None], 0), axis=0)
    arrived, arrived_marks = (
        lax.all_to_all(outgoing, "rows", split_axis=0, concat_axis=0, tiled=True),
        lax.all_to_all(labels, "rows", split_axis=0, concat_axis=0, tiled=True),
    )
    per_row = cols_dev // tile_side
    positions_count = rows_dev // tile_side * per_row
    placement_hot = (
        arrived_marks[:, None] - 1 == jnp.arange(positions_count, dtype=jnp.int32)[None, :]
    ).astype(jnp.bfloat16)
    cell_tiles = jnp.einsum(
        "sp,sc->pc", placement_hot, arrived, preferred_element_type=jnp.float32
    ).astype(jnp.bfloat16)
    density_grid = cell_tiles.reshape(
        rows_dev // tile_side, per_row, tile_side, tile_side
    ).transpose(0, 2, 1, 3)
    density_grid = density_grid.reshape(rows_dev, cols_dev)
    me_col = lax.axis_index("cols")
    highest = lax.Precision.HIGHEST
    slab_cols = cols_dev * cols_n
    zeros_init = jnp.zeros((rows_dev, cols_dev), jnp.float32)
    shard_rows = gathered_copies(density_grid[None], "cols", 0)
    owners = jnp.arange(shard_rows.shape[0], dtype=jnp.int32)
    angles = 2.0 * math.pi / cols_n * (owners * me_col % cols_n).astype(jnp.float32)
    values = shard_rows.astype(jnp.float32)
    sum_real = jnp.tensordot(jnp.cos(angles), values, axes=1, precision=highest)
    sum_imag = (zeros_init, zeros_init)[1] - jnp.tensordot(
        jnp.sin(angles), values, axes=1, precision=highest
    )
    columns = jnp.arange(cols_dev, dtype=jnp.int32)[None, :]
    real_part, imag_part = twiddle(sum_real, sum_imag, columns, me_col, slab_cols)
    section_one = jnp.concatenate([real_part, imag_part], 1).astype(jnp.bfloat16)
    row_table = make_table(cols_dev, 1.0 / math.sqrt(slab_cols)).reshape(2 * cols_dev, 2 * cols_dev)
    rows_spectrum = jnp.dot(section_one, row_table, preferred_element_type=jnp.float32).astype(
        jnp.bfloat16
    )
    rows_spectrum = rows_spectrum.reshape(rows_dev, 2, cols_dev)
    me_row = lax.axis_index("rows")
    group_rows = rows_dev // rows_n
    grid_rows = rows_dev * rows_n
    col_table = make_table(rows_n, 1.0).transpose(3, 2, 1, 0)
    column_block = lax.all_to_all(rows_spectrum, "rows", split_axis=0, concat_axis=0, tiled=True)
    item_width = column_block.shape[2]
    values = column_block.reshape(rows_n, group_rows, 2, item_width)
    combined = jnp.einsum("kqap,atpc->ktqc", col_table, values, preferred_element_type=jnp.float32)
    row_index = (me_row * group_rows + jnp.arange(group_rows, dtype=jnp.int32))[None, :, None]
    row_freq = jnp.arange(rows_n, dtype=jnp.int32)[:, None, None]
    real_two, imag_two = twiddle(
        combined[:, :, 0], combined[:, :, 1], row_index, row_freq, grid_rows
    )
    section_two = lax.all_to_all(
        jnp.stack([real_two, imag_two], 2).astype(jnp.bfloat16).reshape(rows_dev, 2, item_width),
        "rows",
        split_axis=0,
        concat_axis=0,
        tiled=True,
    )
    final_table = (
        make_table(rows_dev, 1.0 / math.sqrt(grid_rows))
        .transpose(3, 2, 1, 0)
        .reshape(2 * rows_dev, 2 * rows_dev)
    )
    result_spec = jnp.dot(
        final_table, section_two.reshape(2 * rows_dev, cols_dev), preferred_element_type=jnp.float32
    )
    result_spec = result_spec.reshape(rows_dev, 2, cols_dev)
    return result_spec * psf_spectrum.astype(jnp.float32)[:, None, :]


def solution(mesh):
    in_specs = (
        P(("rows", "cols"), None, None),
        P(("rows", "cols"), None),
        P(("rows", "cols")),
        P("rows", "cols"),
    )
    out_specs = P("rows", None, "cols")
    return jax.shard_map(
        on_device, mesh=mesh, in_specs=in_specs, out_specs=out_specs, check_vma=False
    )
```

profile of v0, /device:TPU:1, one launch (start us, length us, event | category | flops | bytes accessed | tf_op | source)
XLA Modules:
  0.0 260.7 jit_solution(11228896958120956154)
XLA Ops:
  0.0 0.7 fusion.43
  0.8 0.8 select_reduce_fusion.1
  1.7 0.7 fusion.55
  2.3 0.7 broadcast_add_fusion
  3.1 0.8 all_to_all.23
  3.9 20.4 %all-to-all-start = ((s32[128,2,1]{1,2,0:T(1,128)}), s32[128,2,1]{1,2,0:T(1,128)S(1)}, u32[]{:S(2)}, u32[]{:S(2)}) async-start(s32[128,2,1]{1,2,0:T(1,128)} %bitcast.8), calls=%async_computation | async-start | bytes 131072 | tf_op jit(solution)/shard_map/all_to_all | solution.py:65
  24.3 2.1 reshape.383
  26.3 0.8 convolution_convert_fusion
  27.1 2.6 %all_to_all.25 = bf16[128,2,4096]{2,1,0:T(2,128)(2,1)} reshape(bf16[256,4096]{1,0:T(8,128)(2,1)S(1)} %convolution_convert_fusion) | data formatting | bytes 4194304 | tf_op jit(solution)/shard_map/all_to_all | solution.py:64
  29.8 9.3 %all-to-all-done = s32[128,2,1]{1,2,0:T(1,128)S(1)} async-done(((s32[128,2,1]{1,2,0:T(1,128)}), s32[128,2,1]{1,2,0:T(1,128)S(1)}, u32[]{:S(2)}, u32[]{:S(2)}) %all-to-all-start) | async-done | bytes 1056 | tf_op jit(solution)/shard_map/all_to_all | solution.py:65
  39.1 6.8 %all-to-all-start.1 = ((bf16[128,2,4096]{2,1,0:T(2,128)(2,1)}), bf16[128,2,4096]{2,1,0:T(2,128)(2,1)S(1)}, u32[]{:S(2)}, u32[]{:S(2)}) async-start(bf16[128,2,4096]{2,1,0:T(2,128)(2,1)} %all_to_all.25), calls=%async_computation.1 | async-start | bytes 4194304 | tf_op jit(solution)/shard_map/all_to_all | solution.py:64
  46.2 95.6 %all-to-all-done.1 = bf16[128,2,4096]{2,1,0:T(2,128)(2,1)S(1)} async-done(((bf16[128,2,4096]{2,1,0:T(2,128)(2,1)}), bf16[128,2,4096]{2,1,0:T(2,128)(2,1)S(1)}, u32[]{:S(2)}, u32[]{:S(2)}) %all-to-all-start.1) | async-done | bytes 2097184 | tf_op jit(solution)/shard_map/all_to_all | solution.py:64
  141.8 2.2 all_to_all.27
  144.0 2.1 convolution_convert_fusion.1
  147.4 1.1 broadcast_in_dim.21
  148.4 4.2 %all-to-all-start.2 = ((bf16[4,1,256,512]{3,2,1,0:T(8,128)(2,1)}), bf16[4,1,256,512]{3,2,1,0:T(8,128)(2,1)S(1)}, u32[]{:S(2)}, u32[]{:S(2)}) async-start(bf16[4,1,256,512]{3,2,1,0:T(8,128)(2,1)} %broadcast_in_dim.21), calls=%async_computation.2 | async-start | bytes 2097152 | tf_op jit(solution)/shard_map/all_to_all | solution.py:17
  152.6 4.0 %fusion.7 = bf16[512,1,512]{2,0,1:T(8,128)(2,1)S(1)} fusion(), kind=kLoop, calls=%fused_computation.21 | loop fusion | flops 4194304 | bytes 524288 | tf_op jit(solution)/shard_map/convert.15
  156.6 4.4 %negate_convert_fusion = (bf16[512,1,512]{2,0,1:T(8,128)(2,1)S(1)}, bf16[512,1,512]{2,0,1:T(8,128)(2,1)S(1)}) fusion(), kind=kLoop, calls=%fused_computation.15 | loop fusion | flops 4980736 | bytes 1048576 | tf_op jit(solution)/shard_map/convert.19
  161.4 2.2 copy.48
  163.6 0.6 copy.64
  164.2 2.0 fusion.10
  166.2 2.0 fusion.8
  168.4 0.7 convolution_convert_fusion.2
  169.1 1.2 reshape.386
  170.3 14.8 %all-to-all-start.3 = ((bf16[256,2,512]{2,1,0:T(2,128)(2,1)}), bf16[256,2,512]{2,1,0:T(2,128)(2,1)S(1)}, u32[]{:S(2)}, u32[]{:S(2)}) async-start(bf16[256,2,512]{2,1,0:T(2,128)(2,1)} %reshape.386), calls=%async_computation.3 | async-start | bytes 1048576 | tf_op jit(solution)/shard_map/all_to_all | solution.py:103
  185.8 30.0 %all-to-all-done.3 = bf16[256,2,512]{2,1,0:T(2,128)(2,1)S(1)} async-done(((bf16[256,2,512]{2,1,0:T(2,128)(2,1)}), bf16[256,2,512]{2,1,0:T(2,128)(2,1)S(1)}, u32[]{:S(2)}, u32[]{:S(2)}) %all-to-all-start.3) | async-done | bytes 524320 | tf_op jit(solution)/shard_map/all_to_all | solution.py:103
  217.2 1.3 copy.53
  218.5 9.2 %all-to-all-start.4 = ((bf16[256,2,512]{2,1,0:T(2,128)(2,1)}), bf16[256,2,512]{2,1,0:T(2,128)(2,1)S(1)}, u32[]{:S(2)}, u32[]{:S(2)}) async-start(bf16[256,2,512]{2,1,0:T(2,128)(2,1)} %copy.53), calls=%async_computation.4 | async-start | bytes 1048576 | tf_op jit(solution)/shard_map/all_to_all | solution.py:112
  227.8 1.0 fusion.30
  228.8 1.1 negate_convert_fusion.1
  230.0 28.5 %all-to-all-done.4 = bf16[256,2,512]{2,1,0:T(2,128)(2,1)S(1)} async-done(((bf16[256,2,512]{2,1,0:T(2,128)(2,1)}), bf16[256,2,512]{2,1,0:T(2,128)(2,1)S(1)}, u32[]{:S(2)}, u32[]{:S(2)}) %all-to-all-start.4) | async-done | bytes 524320 | tf_op jit(solution)/shard_map/all_to_all | solution.py:112
  258.9 1.8 copy.55
  (29 shorter events, 4.9 us)
Async XLA Ops:
  3.9 35.2 %all-to-all-start = ((s32[128,2,1]{1,2,0:T(1,128)}), s32[128,2,1]{1,2,0:T(1,128)S(1)}, u32[]{:S(2)}, u32[]{:S(2)}) async-start(s32[128,2,1]{1,2,0:T(1,128)} %bitcast.8), calls=%async_computation | async-start | bytes 131072 | tf_op jit(solution)/shard_map/all_to_all | solution.py:65
  39.1 102.7 %all-to-all-start.1 = ((bf16[128,2,4096]{2,1,0:T(2,128)(2,1)}), bf16[128,2,4096]{2,1,0:T(2,128)(2,1)S(1)}, u32[]{:S(2)}, u32[]{:S(2)}) async-start(bf16[128,2,4096]{2,1,0:T(2,128)(2,1)} %all_to_all.25), calls=%async_computation.1 | async-start | bytes 4194304 | tf_op jit(solution)/shard_map/all_to_all | solution.py:64
  148.4 15.8 %all-to-all-start.2 = ((bf16[4,1,256,512]{3,2,1,0:T(8,128)(2,1)}), bf16[4,1,256,512]{3,2,1,0:T(8,128)(2,1)S(1)}, u32[]{:S(2)}, u32[]{:S(2)}) async-start(bf16[4,1,256,512]{3,2,1,0:T(8,128)(2,1)} %broadcast_in_dim.21), calls=%async_computation.2 | async-start | bytes 2097152 | tf_op jit(solution)/shard_map/all_to_all | solution.py:17
  170.3 45.5 %all-to-all-start.3 = ((bf16[256,2,512]{2,1,0:T(2,128)(2,1)}), bf16[256,2,512]{2,1,0:T(2,128)(2,1)S(1)}, u32[]{:S(2)}, u32[]{:S(2)}) async-start(bf16[256,2,512]{2,1,0:T(2,128)(2,1)} %reshape.386), calls=%async_computation.3 | async-start | bytes 1048576 | tf_op jit(solution)/shard_map/all_to_all | solution.py:103
  216.7 11.0 %copy-start = (bf16[256,512]{1,0:T(8,128)(2,1)S(1)}, bf16[256,512]{1,0:T(8,128)(2,1)}, u32[]{:S(2)}) copy-start(bf16[256,512]{1,0:T(8,128)(2,1)} %param.7) | copy-start | bytes 786436
  218.5 39.9 %all-to-all-start.4 = ((bf16[256,2,512]{2,1,0:T(2,128)(2,1)}), bf16[256,2,512]{2,1,0:T(2,128)(2,1)S(1)}, u32[]{:S(2)}, u32[]{:S(2)}) async-start(bf16[256,2,512]{2,1,0:T(2,128)(2,1)} %copy.53), calls=%async_computation.4 | async-start | bytes 1048576 | tf_op jit(solution)/shard_map/all_to_all | solution.py:112
where the time goes:
time: 263 us; the launch traced here: 261 us
  waiting for transfers between devices  163 us (62%)
  starting transfers between devices  55.4 us (21%)
  local copies, waits for them, and re-layouts  17.8 us (7%)
  other arithmetic  15.3 us (6%)
  matrix products  8.46 us (3%)
    all_to_all x1, waiting for transfers between devices, on_device(): lax.all_to_all(outgoing, 'rows', split_axis=0, concat_axis=0, tiled=True)  95.6 us
    all_to_all x1, waiting for transfers between devices, on_device(): lax.all_to_all(rows_spectrum, 'rows', split_axis=0, concat_axis=0, tiled=...  30 us
    all_to_all x1, waiting for transfers between devices, on_device(): lax.all_to_all(jnp.stack([real_two, imag_two], 2).astype(jnp.bfloat16).re...  28.5 us
    all_to_all x1, starting transfers between devices, on_device(): lax.all_to_all(labels, 'rows', split_axis=0, concat_axis=0, tiled=True)  20.4 us
    all_to_all x1, starting transfers between devices, on_device(): lax.all_to_all(rows_spectrum, 'rows', split_axis=0, concat_axis=0, tiled=...  14.8 us
    another operation x8, other arithmetic  11.4 us
    all_to_all x1, waiting for transfers between devices, on_device(): lax.all_to_all(labels, 'rows', split_axis=0, concat_axis=0, tiled=True)  9.31 us
    all_to_all x1, starting transfers between devices, on_device(): lax.all_to_all(jnp.stack([real_two, imag_two], 2).astype(jnp.bfloat16).re...  9.23 us
  transfers between devices with their start and end apart: 5, of which 4 were waited for; matrix products, arithmetic and copies ran while one was open for 7% of the time, Pallas kernels for 0%

commit v1 on v0

v1 whole, which is shorter than its diff:
```python
import math

import jax
import jax.numpy as jnp
from jax import lax
from jax.experimental import pallas as pl
from jax.experimental.pallas import tpu as pltpu
from jax.sharding import Mesh
from jax.sharding import PartitionSpec as P

ROWS = ("chip", "core")
GROUP = ("core", "cols")
F32 = jnp.float32
BF16 = jnp.bfloat16


def table_parts(inputs, outputs, length, factor):
    angles = 2.0 * math.pi / length * (inputs * outputs % length).astype(F32)
    return jnp.cos(angles) * factor, jnp.sin(angles) * factor


def twiddle_parts(position, frequency, period):
    angles = 2.0 * math.pi / period * (position * frequency % period).astype(F32)
    return jnp.cos(angles), jnp.sin(angles)


def lane_group(shape):
    return lax.broadcasted_iota(jnp.int32, shape, 1) // 32


def pack_body(tiles_ref, out_ref):
    group = lane_group((16, 128))
    for block in range(tiles_ref.shape[1] // 128):
        parts = [
            tiles_ref[16 * g : 16 * g + 16, 128 * block : 128 * block + 128].astype(F32)
            for g in range(4)
        ]
        for quarter in range(4):
            value = None
            for g in range(4):
                shift = 32 * ((g - quarter) % 4)
                moved = pltpu.roll(parts[g], shift, 1) if shift else parts[g]
                value = moved if value is None else jnp.where(group == g, moved, value)
            out_ref[4 * block + quarter] = value.astype(BF16)


def scatter_body(slab_hot_ref, place_ref, tiles_ref, out_ref, spread_ref, sum_ref):
    step = pl.program_id(0)
    rows = tiles_ref.shape[0]
    values = tiles_ref[...].astype(F32)
    group = lane_group(values.shape)
    rolls = [values] + [pltpu.roll(values, 32 * j, 1) for j in range(1, 4)]
    total = None
    for g in range(4):
        copies = rolls[(-g) % 4]
        for h in range(1, 4):
            copies = jnp.where(group == h, rolls[(h - g) % 4], copies)
        copies = copies.astype(BF16)
        place = place_ref[:, 128 * g : 128 * g + 128]
        for m in range(8):
            spread_ref[g, :, 128 * m : 128 * m + 128] = jnp.where(
                place == jnp.array(4.0 * m, BF16), copies, jnp.zeros_like(copies)
            )
        part = jnp.dot(slab_hot_ref[g], spread_ref[g], preferred_element_type=F32)
        total = part if total is None else total + part

    @pl.when(step == 0)
    def _():
        sum_ref[...] = total

    @pl.when(step > 0)
    def _():
        sum_ref[...] += total

    @pl.when(step == pl.num_programs(0) - 1)
    def _():
        out_ref[...] = sum_ref[...].astype(BF16)


def rows_body(mix_ref, cells_ref, turn_ref, row_table_ref, slab_table_ref, phase_ref, out_ref):
    halves = []
    for low in range(2):
        real, imag = [], []
        for core in range(2):
            parts = [
                cells_ref[4 * core + e, :, 256 * low : 256 * low + 256].astype(F32)
                for e in range(4)
            ]
            sum_real = parts[0] * mix_ref[0]
            sum_imag = -(parts[0] * mix_ref[4])
            for e in range(1, 4):
                sum_real = sum_real + parts[e] * mix_ref[e]
                sum_imag = sum_imag - parts[e] * mix_ref[4 + e]
            cosine = turn_ref[0:1, 256 * core : 256 * core + 256]
            sine = turn_ref[1:2, 256 * core : 256 * core + 256]
            real.append(sum_real * cosine + sum_imag * sine)
            imag.append(sum_imag * cosine - sum_real * sine)
        halves.append(jnp.concatenate(real + imag, 1).astype(BF16))
    spectrum = jnp.dot(
        jnp.concatenate(halves, 0), row_table_ref[...], preferred_element_type=F32
    ).astype(BF16)
    for low in range(2):
        half = spectrum[128 * low : 128 * low + 128]
        stacked = jnp.concatenate([half[:, :512], half[:, 512:]], 0)
        combined = jnp.dot(slab_table_ref[...], stacked, preferred_element_type=F32)
        cosine = phase_ref[:, 2 * low : 2 * low + 1]
        sine = phase_ref[:, 2 * low + 1 : 2 * low + 2]
        real, imag = combined[:128], combined[128:]
        out_ref[2 * low] = (real * cosine + imag * sine).astype(BF16)
        out_ref[2 * low + 1] = (imag * cosine - real * sine).astype(BF16)


def whole(shape, space=pltpu.VMEM):
    return pl.BlockSpec(shape, lambda *_: (0,) * len(shape), memory_space=space)


def on_device(tile_density, tile_dest, tile_place, psf_spectrum):
    chip = lax.axis_index("chip")
    core = lax.axis_index("core")
    me_col = lax.axis_index("cols")
    iota = lambda n: jnp.arange(n, dtype=jnp.int32)

    tiles_flat = tile_density.reshape(64, 4096)
    outgoing = pl.pallas_call(
        pack_body, out_shape=jax.ShapeDtypeStruct((128, 16, 128), BF16)
    )(tiles_flat)
    arrived = lax.all_to_all(outgoing, ROWS, 0, 0, tiled=True)
    codes = tile_dest[:, 0] * 32 + tile_place
    labels = lax.all_to_all(jnp.broadcast_to(codes[None], (128, 64)), ROWS, 0, 0, tiled=True)

    slabs = (labels // 32).reshape(128, 4, 16).transpose(1, 0, 2).reshape(4, 1, 2048)
    slab_hot = (slabs == iota(128)[None, :, None]).astype(BF16)
    places = (labels % 32).reshape(128, 4, 16).transpose(0, 2, 1).reshape(2048, 4, 1)
    places = (places - (iota(128) // 32)[None, None, :]).astype(BF16).reshape(2048, 512)

    step_rows = 256
    grid_cells = pl.pallas_call(
        scatter_body,
        grid=(2048 // step_rows,),
        in_specs=[
            pl.BlockSpec((4, 128, step_rows), lambda i: (0, 0, i)),
            pl.BlockSpec((step_rows, 512), lambda i: (i, 0)),
            pl.BlockSpec((step_rows, 128), lambda i: (i, 0)),
        ],
        out_specs=pl.BlockSpec((128, 1024), lambda i: (0, 0)),
        out_shape=jax.ShapeDtypeStruct((128, 1024), BF16),
        scratch_shapes=[
            pltpu.VMEM((4, step_rows, 1024), BF16),
            pltpu.VMEM((128, 1024), F32),
        ],
    )(slab_hot, places, arrived.reshape(2048, 128))

    halves = jnp.stack([grid_cells[:, :512], grid_cells[:, 512:]], 0)
    sent = jnp.broadcast_to(halves[:, None], (2, 4, 128, 512)).reshape(8, 128, 512)
    cells = lax.all_to_all(sent, GROUP, 0, 0, tiled=True)

    order = iota(512)
    column = order % 256 // 32 * 64 + order // 256 * 32 + order % 32
    cosine, sine = table_parts(
        column[:, None], iota(512)[None, :], 512, 1.0 / math.sqrt(2048)
    )
    row_table = jnp.concatenate(
        [jnp.concatenate([cosine, -sine], 1), jnp.concatenate([sine, cosine], 1)], 0
    ).astype(BF16)
    cosine, sine = table_parts(iota(128)[:, None], iota(128)[None, :], 128, 1.0)
    slab_table = jnp.concatenate(
        [jnp.concatenate([cosine, sine], 1), jnp.concatenate([-sine, cosine], 1)], 0
    ).astype(BF16)
    angles = 2.0 * math.pi / 4 * (iota(4) * me_col % 4).astype(F32)
    mix = jnp.concatenate([jnp.cos(angles), jnp.sin(angles)])
    turn = jnp.stack(twiddle_parts(column, me_col, 2048), 0)
    phases = []
    for low in range(2):
        phases += twiddle_parts(64 * (2 * core + low) + chip, iota(128), 32768)
    phase = jnp.stack(phases, 1)

    section_two = pl.pallas_call(
        rows_body,
        in_specs=[
            pl.BlockSpec(memory_space=pltpu.SMEM),
            whole((8, 128, 512)),
            whole((2, 512)),
            whole((1024, 1024)),
            whole((256, 256)),
            whole((128, 4)),
        ],
        out_specs=whole((4, 128, 512)),
        out_shape=jax.ShapeDtypeStruct((4, 128, 512), BF16),
    )(mix, cells, turn, row_table, slab_table, phase)

    section_two = lax.all_to_all(
        section_two.transpose(1, 0, 2), ROWS, split_axis=0, concat_axis=0, tiled=True
    )

    place = iota(256)
    position = 64 * (place % 4) + place // 4
    cosine, sine = table_parts(
        iota(256)[:, None], position[None, :], 256, 1.0 / math.sqrt(32768)
    )
    final_table = jnp.stack(
        [jnp.stack([cosine, sine], 2), jnp.stack([-sine, cosine], 2)], 1
    ).reshape(512, 512).astype(BF16)
    result = jnp.dot(final_table, section_two.reshape(512, 512), preferred_element_type=F32)
    return result.reshape(256, 2, 512) * psf_spectrum.astype(F32)[:, None, :]


def solution(mesh):
    split = Mesh(
        mesh.devices.reshape(mesh.devices.shape[0] // 2, 2, mesh.devices.shape[1]),
        ("chip", "core", "cols"),
    )
    everywhere = ("chip", "core", "cols")
    in_specs = (P(everywhere, None, None), P(everywhere, None), P(everywhere), P(ROWS, "cols"))
    return jax.shard_map(
        on_device,
        mesh=split,
        in_specs=in_specs,
        out_specs=P(ROWS, None, "cols"),
        check_vma=False,
    )
```

time: 263 us -> 159 us (0.60)
  waiting for transfers between devices: 163 us -> 64 us
  Pallas kernels: 0 us -> 16.7 us
  starting transfers between devices: 55.4 us -> 40.7 us
  matrix products: 8.46 us -> 0.44 us
    all_to_all x5 -> x4, waiting for transfers between devices: 163 us -> 64 us  [the longest x1 28.5 us: on_device(): lax.all_to_all(section_two.transpose(1, 0, 2), ROWS, split_axis=0, concat...]
    pallas_call x0 -> x3, Pallas kernels: none -> 16.7 us  [the longest x1 10.3 us: on_device(): pl.pallas_call(scatter_body, grid=(2048 // step_rows,), in_specs=[pl.Bloc...]
    all_to_all x5 -> x4, starting transfers between devices: 55.4 us -> 40.7 us  [the longest x1 20.4 us: on_device(): lax.all_to_all(jnp.broadcast_to(codes[None], (128, 64)), ROWS, 0, 0, tile...]
    dot_general x7 -> x1, matrix products: 8.46 us -> 0.44 us  [on_device(): jnp.dot(final_table, section_two.reshape(512, 512), preferred_element_typ...]
    all_to_all x3 -> x1, local copies, waits for them, and re-layouts: 5.61 us -> 0.06 us  [on_device(): lax.all_to_all(jnp.broadcast_to(codes[None], (128, 64)), ROWS, 0, 0, tile...]
    sub x1 -> x3, local copies, waits for them, and re-layouts: 0.14 us -> 5.66 us  [on_device(): places - (iota(128) // 32)[None, None, :]]
    another operation x14 -> x8, other arithmetic: 11.9 us -> 7.32 us
    convert_element_type x2 -> x3, other arithmetic: 0.78 us -> 3.87 us  [the longest x1 1.92 us: on_device(): (places - (iota(128) // 32)[None, None, :]).astype(BF16).reshape(2048, 512)]
  transfers between devices with their start and end apart: 5 -> 4, of which waited for: 4 -> 4; matrix products, arithmetic and copies ran while one was open for 7% -> 16% of each run, Pallas kernels for 0% -> 1%
where the time goes in v1:
time: 159 us; the launch traced here: 156 us
  waiting for transfers between devices  64 us (40%)
  starting transfers between devices  40.7 us (26%)
  local copies, waits for them, and re-layouts  19 us (12%)
  Pallas kernels  16.7 us (11%)
  other arithmetic  15.2 us (10%)
    all_to_all x1, waiting for transfers between devices, on_device(): lax.all_to_all(section_two.transpose(1, 0, 2), ROWS, split_axis=0, concat...  28.5 us
    all_to_all x1, waiting for transfers between devices, on_device(): arrived = lax.all_to_all(outgoing, ROWS, 0, 0, tiled=True)  20.6 us
    all_to_all x1, starting transfers between devices, on_device(): lax.all_to_all(jnp.broadcast_to(codes[None], (128, 64)), ROWS, 0, 0, tile...  20.4 us
    pallas_call x1, Pallas kernels, on_device(): pl.pallas_call(scatter_body, grid=(2048 // step_rows,), in_specs=[pl.Bloc...  10.3 us
    all_to_all x1, waiting for transfers between devices, on_device(): lax.all_to_all(jnp.broadcast_to(codes[None], (128, 64)), ROWS, 0, 0, tile...  9.78 us
    all_to_all x1, starting transfers between devices, on_device(): lax.all_to_all(section_two.transpose(1, 0, 2), ROWS, split_axis=0, concat...  8.43 us
    another operation x4, other arithmetic  6.65 us
    all_to_all x1, starting transfers between devices, on_device(): arrived = lax.all_to_all(outgoing, ROWS, 0, 0, tiled=True)  6.35 us
  transfers between devices with their start and end apart: 4, of which 4 were waited for; matrix products, arithmetic and copies ran while one was open for 16% of the time, Pallas kernels for 1%

profile of v1, /device:TPU:1, one launch (start us, length us, event | category | flops | bytes accessed | tf_op | source)
XLA Modules:
  0.0 156.2 jit_solution(11839932293038192201)
XLA Ops:
  0.0 0.7 bitcast_add_fusion
  0.7 0.6 broadcast_in_dim.4
  1.3 20.4 %all-to-all-start = ((s32[128,1,64]{2,1,0:T(1,128)}), s32[128,1,64]{2,1,0:T(1,128)S(1)}, u32[]{:S(2)}, u32[]{:S(2)}) async-start(s32[128,1,64]{2,1,0:T(1,128)} %broadcast_in_dim.4), calls=%async_computation | async-start | bytes 131072 | tf_op jit(solution)/shard_map/all_to_all | solution.py:129
  21.8 2.7 %reshape.535.tiles_ref = bf16[64,4096]{1,0:T(8,128)(2,1)} reshape(bf16[64,64,64]{2,1,0:T(8,128)(2,1)} %param.4) | data formatting | bytes 1048576 | tf_op jit(solution)/shard_map/reshape | solution.py:123
  24.5 2.3 %shard_map.46 = bf16[128,16,128]{2,1,0:T(8,128)(2,1)} custom-call(bf16[64,4096]{1,0:T(8,128)(2,1)} %reshape.535.tiles_ref), custom_call_target="tpu_custom_call" | custom-call | tf_op jit(solution)/shard_map/pallas_call | solution.py:124
  26.9 9.8 %all-to-all-done = s32[128,1,64]{2,1,0:T(1,128)S(1)} async-done(((s32[128,1,64]{2,1,0:T(1,128)}), s32[128,1,64]{2,1,0:T(1,128)S(1)}, u32[]{:S(2)}, u32[]{:S(2)}) %all-to-all-start) | async-done | bytes 32800 | tf_op jit(solution)/shard_map/all_to_all | solution.py:129
  36.7 6.3 %all-to-all-start.1 = ((bf16[128,16,128]{2,1,0:T(8,128)(2,1)}), bf16[128,16,128]{2,1,0:T(8,128)(2,1)S(1)}, u32[]{:S(2)}, u32[]{:S(2)}) async-start(bf16[128,16,128]{2,1,0:T(8,128)(2,1)} %shard_map.46), calls=%async_computation.1 | async-start | bytes 1048576 | tf_op jit(solution)/shard_map/all_to_all | solution.py:127
  43.3 0.5 copy.39
  44.2 1.9 %fusion.1.slab_hot_ref = bf16[4,128,2048]{2,1,0:T(8,128)(2,1)} fusion(s32[4,2048]{1,0:T(4,128)S(1)} %eq.34), kind=kLoop, calls=%fused_computation.3 | loop fusion | flops 2097152 | bytes 2129920 | tf_op jit(solution)/shard_map/convert_element_type | solution.py:132
  46.1 5.1 %sub.75 = s32[2048,4,128]{2,1,0:T(4,128)S(1)} broadcast(s32[2048,4]{1,0:T(8,128)S(1)} %bitcast.28), dimensions={0,1} | broadcast | bytes 4227072 | tf_op jit(solution)/shard_map/sub | solution.py:134
  51.2 1.9 %fusion.place_ref = bf16[2048,512]{1,0:T(8,128)(2,1)} fusion(s32[256,8,4,128]{3,2,1,0:T(4,128)S(1)} %bitcast.27, s32[512]{0:T(512)S(1)} %broadcast_bitcast_fusion), kind=kLoop, calls=%fused_computation.1 | loop fusion | flops 2097152 | bytes 6293504 | tf_op jit(solution)/shard_map/convert_element_type | solution.py:134
  53.1 20.6 %all-to-all-done.1 = bf16[128,16,128]{2,1,0:T(8,128)(2,1)S(1)} async-done(((bf16[128,16,128]{2,1,0:T(8,128)(2,1)}), bf16[128,16,128]{2,1,0:T(8,128)(2,1)S(1)}, u32[]{:S(2)}, u32[]{:S(2)}) %all-to-all-start.1) | async-done | bytes 524320 | tf_op jit(solution)/shard_map/all_to_all | solution.py:127
  73.7 0.8 copy-done.1
  74.5 10.3 %shard_map.47 = bf16[128,1024]{1,0:T(8,128)(2,1)} custom-call(bf16[4,128,2048]{2,1,0:T(8,128)(2,1)} %fusion.1.slab_hot_ref, bf16[2048,512]{1,0:T(8,128)(2,1)} %fusion.place_ref, bf16[2048,128]{1,0:T(8,128)(2,1)} %bitcast.29), custom_call_target="tpu_custom_call" | custom-call | tf_op jit(solution)/shard_map/pallas_call | solution.py:137
  84.8 1.0 slice_bitcast_fusion.1
  85.9 1.1 broadcast_in_dim.5
  86.9 5.6 %all-to-all-start.2 = ((bf16[8,128,512]{2,1,0:T(8,128)(2,1)}), bf16[8,128,512]{2,1,0:T(8,128)(2,1)S(1)}, u32[]{:S(2)}, u32[]{:S(2)}) async-start(bf16[8,128,512]{2,1,0:T(8,128)(2,1)} %bitcast.9), calls=%async_computation.2 | async-start | bytes 2097152 | tf_op jit(solution)/shard_map/all_to_all | solution.py:155
  92.5 0.7 pad_maximum_fusion.5.mix_ref
  93.2 0.7 copy.36.phase_ref
  93.9 0.6 pad_maximum_fusion.3.turn_ref
  95.0 0.7 maximum_maximum_fusion.1.slab_table_ref
  95.7 5.0 %negate_convert_fusion = (bf16[512,512]{1,0:T(8,128)(2,1)S(1)}, bf16[512,512]{1,0:T(8,128)(2,1)S(1)}, bf16[512,512]{1,0:T(8,128)(2,1)S(1)}) fusion(s32[512]{0:T(512)S(1)} %fusion.43), kind=kLoop, calls=%fused_computation.12 | loop fusion | flops 5242880 | bytes 1574912 | tf_op jit(solution)/shard_map/convert.11
  100.7 1.7 %maximum_maximum_fusion.row_table_ref = bf16[1024,1024]{1,0:T(8,128)(2,1)} fusion(bf16[512,512]{1,0:T(8,128)(2,1)S(1)} %get-tuple-element.13, bf16[512,512]{1,0:T(8,128)(2,1)S(1)} %get-tuple-element.12, bf16[512,512]{1,0:T(8,128)(2,1)S(1)} %get-tuple-element.11), kind=kLoop, calls=%fused_computation.4 | loop fusion | flops 8388608 | bytes 3670016 | tf_op jit(solution)/shard_map/concatenate | solution.py:162
  102.3 5.1 %all-to-all-done.2.cells_ref = bf16[8,128,512]{2,1,0:T(8,128)(2,1)S(1)} async-done(((bf16[8,128,512]{2,1,0:T(8,128)(2,1)}), bf16[8,128,512]{2,1,0:T(8,128)(2,1)S(1)}, u32[]{:S(2)}, u32[]{:S(2)}) %all-to-all-start.2) | async-done | bytes 1048608 | tf_op jit(solution)/shard_map/all_to_all | solution.py:155
  107.4 1.0 copy-done
  108.4 4.1 %shard_map.48 = bf16[4,128,512]{2,1,0:T(8,128)(2,1)} custom-call(f32[8]{0:T(128)} %pad_maximum_fusion.5.mix_ref, bf16[8,128,512]{2,1,0:T(8,128)(2,1)} %copy-done, f32[2,512]{1,0:T(2,128)} %pad_maximum_fusion.3.turn_ref, bf16[1024,1024]{1,0:T(8,128)(2,1)} %maximum_maximum_fusion.row_table_ref, bf16[256,256]{1,0:T(8,128)(2,1)} %maximum_maximum_fusion.1.slab_table_ref, ...), custom_call_target="tpu_custom_call" | custom-call | tf_op jit(solution)/shard_map/pallas_call | solution.py:177
  112.5 2.3 %copy.37 = bf16[128,4,512]{2,1,0:T(4,128)(2,1)} copy(bf16[128,4,512]{2,0,1:T(8,128)(2,1)} %bitcast.30) | data formatting | bytes 1048576 | tf_op jit(solution)/shard_map/transpose | solution.py:192
  114.8 8.4 %all-to-all-start.3 = ((bf16[128,4,512]{2,1,0:T(4,128)(2,1)}), bf16[128,4,512]{2,1,0:T(4,128)(2,1)S(1)}, u32[]{:S(2)}, u32[]{:S(2)}) async-start(bf16[128,4,512]{2,1,0:T(4,128)(2,1)} %copy.37), calls=%async_computation.3 | async-start | bytes 1048576 | tf_op jit(solution)/shard_map/all_to_all | solution.py:191
  123.2 1.2 fusion.18
  125.4 28.5 %all-to-all-done.3 = bf16[128,4,512]{2,1,0:T(4,128)(2,1)S(1)} async-done(((bf16[128,4,512]{2,1,0:T(4,128)(2,1)}), bf16[128,4,512]{2,1,0:T(4,128)(2,1)S(1)}, u32[]{:S(2)}, u32[]{:S(2)}) %all-to-all-start.3) | async-done | bytes 524320 | tf_op jit(solution)/shard_map/all_to_all | solution.py:191
  154.0 0.4 convolution_multiply_fusion
  154.4 1.8 %copy.38 = f32[256,2,512]{2,1,0:T(2,128)} copy(f32[256,2,512]{2,0,1:T(8,128)S(1)} %convolution_multiply_fusion) | data formatting | bytes 2097152 | tf_op jit(solution)/shard_map/mul | solution.py:204
  (29 shorter events, 2.3 us)
Async XLA Ops:
  1.3 35.3 %all-to-all-start = ((s32[128,1,64]{2,1,0:T(1,128)}), s32[128,1,64]{2,1,0:T(1,128)S(1)}, u32[]{:S(2)}, u32[]{:S(2)}) async-start(s32[128,1,64]{2,1,0:T(1,128)} %broadcast_in_dim.4), calls=%async_computation | async-start | bytes 131072 | tf_op jit(solution)/shard_map/all_to_all | solution.py:129
  36.7 37.0 %all-to-all-start.1 = ((bf16[128,16,128]{2,1,0:T(8,128)(2,1)}), bf16[128,16,128]{2,1,0:T(8,128)(2,1)S(1)}, u32[]{:S(2)}, u32[]{:S(2)}) async-start(bf16[128,16,128]{2,1,0:T(8,128)(2,1)} %shard_map.46), calls=%async_computation.1 | async-start | bytes 1048576 | tf_op jit(solution)/shard_map/all_to_all | solution.py:127
  73.7 0.8 copy-start.1
  86.9 20.5 %all-to-all-start.2 = ((bf16[8,128,512]{2,1,0:T(8,128)(2,1)}), bf16[8,128,512]{2,1,0:T(8,128)(2,1)S(1)}, u32[]{:S(2)}, u32[]{:S(2)}) async-start(bf16[8,128,512]{2,1,0:T(8,128)(2,1)} %bitcast.9), calls=%async_computation.2 | async-start | bytes 2097152 | tf_op jit(solution)/shard_map/all_to_all | solution.py:155
  107.4 1.0 copy-start
  112.5 12.8 %copy-start.2 = (bf16[256,512]{1,0:T(8,128)(2,1)S(1)}, bf16[256,512]{1,0:T(8,128)(2,1)}, u32[]{:S(2)}) copy-start(bf16[256,512]{1,0:T(8,128)(2,1)} %param.7) | copy-start | bytes 786436
  114.8 39.1 %all-to-all-start.3 = ((bf16[128,4,512]{2,1,0:T(4,128)(2,1)}), bf16[128,4,512]{2,1,0:T(4,128)(2,1)S(1)}, u32[]{:S(2)}, u32[]{:S(2)}) async-start(bf16[128,4,512]{2,1,0:T(4,128)(2,1)} %copy.37), calls=%async_computation.3 | async-start | bytes 1048576 | tf_op jit(solution)/shard_map/all_to_all | solution.py:191

commit v2 on v1

v2 whole, which is shorter than its diff:
```python
import math

import jax
import jax.numpy as jnp
from jax import lax
from jax.experimental import pallas as pl
from jax.experimental.pallas import tpu as pltpu
from jax.sharding import Mesh
from jax.sharding import PartitionSpec as P

ROWS = ("chip", "core")
GROUP = ("core", "cols")
F32 = jnp.float32
BF16 = jnp.bfloat16


def table_parts(inputs, outputs, length, factor):
    angles = 2.0 * math.pi / length * (inputs * outputs % length).astype(F32)
    return jnp.cos(angles) * factor, jnp.sin(angles) * factor


def twiddle_parts(position, frequency, period):
    angles = 2.0 * math.pi / period * (position * frequency % period).astype(F32)
    return jnp.cos(angles), jnp.sin(angles)


def lane_group(shape):
    return lax.broadcasted_iota(jnp.int32, shape, 1) // 32


def pack_body(tiles_ref, dest_ref, place_ref, out_ref, flat_ref, packed_ref):
    for part in range(4):
        flat_ref[1024 * part : 1024 * part + 1024, :64] = (
            tiles_ref[16 * part : 16 * part + 16].reshape(1024, 64).astype(F32)
        )
    place = place_ref[...]
    labels = jnp.concatenate([place // 16 * 128 + dest_ref[...], place % 16], 1)
    labels = jnp.broadcast_to(labels.astype(F32), (2, 128))
    group = lane_group((16, 128))
    for chip in range(64):
        parts = [flat_ref[pl.ds(1024 * g + chip, 16, stride=64), :] for g in range(4)]
        for core in range(2):
            value = None
            for g in range(4):
                shift = 32 * (g - core) % 128
                moved = pltpu.roll(parts[g], shift, 1) if shift else parts[g]
                value = moved if value is None else jnp.where(group == g, moved, value)
            start = 18 * (2 * chip + core)
            packed_ref[start : start + 16] = value
            packed_ref[start + 16 : start + 18] = labels
    out_ref[...] = packed_ref[...].astype(BF16)


def scatter_body(tiles_ref, out_ref, flat_ref, spread_ref, hot_ref):
    flat_ref[...] = tiles_ref[...].astype(F32)
    labels = flat_ref[pl.ds(16, 128, stride=18), :]
    named = jnp.transpose(labels)
    group = lane_group((128, 128))
    lane = group.astype(F32)
    slab = lax.broadcasted_iota(jnp.int32, (256, 128), 0).astype(F32)
    total = None
    for step in range(16):
        slot = step % 2
        values = flat_ref[pl.ds(step, 128, stride=18), :]
        rolls = [values] + [pltpu.roll(values, 32 * j, 1) for j in range(1, 4)]
        for g in range(4):
            copies = rolls[(-g) % 4]
            for h in range(1, 4):
                copies = jnp.where(group == h, rolls[(h - g) % 4], copies)
            copies = copies.astype(BF16)
            tile = 16 * g + step
            place = jnp.broadcast_to(labels[:, 64 + tile : 65 + tile], (128, 128)) - lane
            place = place.astype(BF16)
            for m in range(4):
                spread_ref[slot, 128 * g : 128 * g + 128, 128 * m : 128 * m + 128] = jnp.where(
                    place == jnp.array(4.0 * m, BF16), copies, jnp.zeros_like(copies)
                )
            hot = jnp.broadcast_to(named[tile : tile + 1, :], (256, 128)) == slab
            hot_ref[slot, :, 128 * g : 128 * g + 128] = jnp.where(hot, 1.0, 0.0).astype(BF16)
        part = jnp.dot(hot_ref[slot], spread_ref[slot], preferred_element_type=F32)
        total = part if total is None else total + part
    total = total.astype(BF16)
    for core in range(2):
        for e in range(4):
            out_ref[4 * core + e] = total[128 * core : 128 * core + 128]


def rows_body(
    mix_ref, cells_ref, turn_ref, row_table_ref, slab_table_ref, phase_ref, out_ref, flat_ref
):
    halves = []
    for low in range(2):
        real, imag = [], []
        for core in range(2):
            parts = [
                cells_ref[4 * core + e, :, 256 * low : 256 * low + 256].astype(F32)
                for e in range(4)
            ]
            sum_real = parts[0] * mix_ref[0]
            sum_imag = -(parts[0] * mix_ref[4])
            for e in range(1, 4):
                sum_real = sum_real + parts[e] * mix_ref[e]
                sum_imag = sum_imag - parts[e] * mix_ref[4 + e]
            cosine = turn_ref[0:1, 256 * core : 256 * core + 256]
            sine = turn_ref[1:2, 256 * core : 256 * core + 256]
            real.append(sum_real * cosine + sum_imag * sine)
            imag.append(sum_imag * cosine - sum_real * sine)
        halves.append(jnp.concatenate(real + imag, 1).astype(BF16))
    spectrum = jnp.dot(
        jnp.concatenate(halves, 0), row_table_ref[...], preferred_element_type=F32
    ).astype(BF16)
    for low in range(2):
        half = spectrum[128 * low : 128 * low + 128]
        stacked = jnp.concatenate([half[:, :512], half[:, 512:]], 0)
        combined = jnp.dot(slab_table_ref[...], stacked, preferred_element_type=F32)
        cosine = phase_ref[:, 2 * low : 2 * low + 1]
        sine = phase_ref[:, 2 * low + 1 : 2 * low + 2]
        real, imag = combined[:128], combined[128:]
        turned = [real * cosine + imag * sine, imag * cosine - real * sine]
        for p in range(2):
            for v in range(4):
                flat_ref[pl.ds(4 * (2 * low + p) + v, 128, stride=16), :] = turned[p][
                    :, 128 * v : 128 * v + 128
                ]
    out_ref[...] = flat_ref[...].astype(BF16)


VMEM = pl.BlockSpec(memory_space=pltpu.VMEM)
SMEM = pl.BlockSpec(memory_space=pltpu.SMEM)


def on_device(tile_density, tile_dest, tile_place, psf_spectrum):
    chip = lax.axis_index("chip")
    core = lax.axis_index("core")
    me_col = lax.axis_index("cols")
    iota = lambda n: jnp.arange(n, dtype=jnp.int32)

    outgoing = pl.pallas_call(
        pack_body,
        in_specs=[VMEM] * 3,
        out_specs=VMEM,
        out_shape=jax.ShapeDtypeStruct((2304, 128), BF16),
        scratch_shapes=[pltpu.VMEM((4096, 128), F32), pltpu.VMEM((2304, 128), F32)],
    )(tile_density, tile_dest.reshape(1, 64), tile_place.reshape(1, 64))
    arrived = lax.all_to_all(outgoing.reshape(128, 9, 2, 128), ROWS, 0, 0, tiled=True)
    sent = pl.pallas_call(
        scatter_body,
        in_specs=[VMEM],
        out_specs=VMEM,
        out_shape=jax.ShapeDtypeStruct((8, 128, 512), BF16),
        scratch_shapes=[
            pltpu.VMEM((2304, 128), F32),
            pltpu.VMEM((2, 512, 512), BF16),
            pltpu.VMEM((2, 256, 512), BF16),
        ],
    )(pltpu.with_memory_space_constraint(arrived.reshape(2304, 128), pltpu.VMEM))

    cells = lax.all_to_all(sent, GROUP, 0, 0, tiled=True)
    cells = pltpu.with_memory_space_constraint(cells, pltpu.VMEM)

    order = iota(512)
    column = order % 256 // 32 * 64 + order // 256 * 32 + order % 32
    cosine, sine = table_parts(
        column[:, None], iota(512)[None, :], 512, 1.0 / math.sqrt(2048)
    )
    row_table = jnp.concatenate(
        [jnp.concatenate([cosine, -sine], 1), jnp.concatenate([sine, cosine], 1)], 0
    ).astype(BF16)
    cosine, sine = table_parts(iota(128)[:, None], iota(128)[None, :], 128, 1.0)
    slab_table = jnp.concatenate(
        [jnp.concatenate([cosine, sine], 1), jnp.concatenate([-sine, cosine], 1)], 0
    ).astype(BF16)
    angles = 2.0 * math.pi / 4 * (iota(4) * me_col % 4).astype(F32)
    mix = jnp.concatenate([jnp.cos(angles), jnp.sin(angles)])
    turn = jnp.stack(twiddle_parts(column, me_col, 2048), 0)
    phases = []
    for low in range(2):
        phases += twiddle_parts(64 * (2 * core + low) + chip, iota(128), 32768)
    phase = jnp.stack(phases, 1)

    section_two = pl.pallas_call(
        rows_body,
        in_specs=[SMEM] + [VMEM] * 5,
        out_specs=VMEM,
        out_shape=jax.ShapeDtypeStruct((2048, 128), BF16),
        scratch_shapes=[pltpu.VMEM((2048, 128), F32)],
    )(
        mix,
        cells,
        turn,
        pltpu.with_memory_space_constraint(row_table, pltpu.VMEM),
        pltpu.with_memory_space_constraint(slab_table, pltpu.VMEM),
        phase,
    )
    section_two = lax.all_to_all(section_two.reshape(128, 16, 128), ROWS, 0, 0, tiled=True)

    place = iota(256)
    position = 64 * (place % 4) + place // 4
    cosine, sine = table_parts(
        iota(256)[:, None], position[None, :], 256, 1.0 / math.sqrt(32768)
    )
    final_table = jnp.stack(
        [jnp.stack([cosine, sine], 2), jnp.stack([-sine, cosine], 2)], 1
    ).reshape(512, 512).astype(BF16)
    section_two = section_two.reshape(512, 512)
    result = jnp.dot(final_table, section_two, preferred_element_type=F32)
    return result.reshape(256, 2, 512) * psf_spectrum.astype(F32)[:, None, :]


def solution(mesh):
    split = Mesh(
        mesh.devices.reshape(mesh.devices.shape[0] // 2, 2, mesh.devices.shape[1]),
        ("chip", "core", "cols"),
    )
    everywhere = ("chip", "core", "cols")
    in_specs = (P(everywhere, None, None), P(everywhere, None), P(everywhere), P(ROWS, "cols"))
    return jax.shard_map(
        on_device,
        mesh=split,
        in_specs=in_specs,
        out_specs=P(ROWS, None, "cols"),
        check_vma=False,
    )
```

time: 159 us -> 131 us (0.82)
  local copies, waits for them, and re-layouts: 19 us -> 3.68 us
  other arithmetic: 15.2 us -> 8.62 us
  starting transfers between devices: 40.7 us -> 34.2 us
  waiting for transfers between devices: 64 us -> 68.9 us
  Pallas kernels: 16.7 us -> 12.2 us
    all_to_all x3 -> x2, starting transfers between devices: 35.2 us -> 28.5 us  [the longest x1 20.4 us: on_device(): lax.all_to_all(outgoing.reshape(128, 9, 2, 128), ROWS, 0, 0, tiled=True)]
    sub x3 -> x0, local copies, waits for them, and re-layouts: 5.66 us -> none  [on_device(): places - (iota(128) // 32)[None, None, :]]
    pallas_call x3, Pallas kernels: 16.7 us -> 12.2 us  [the longest x1 5.18 us: on_device(): pl.pallas_call(scatter_body, in_specs=[VMEM], out_specs=VMEM, out_shape=j...]
    convert_element_type x2 -> x0, other arithmetic: 3.82 us -> none  [the longest x1 1.92 us: on_device(): (places - (iota(128) // 32)[None, None, :]).astype(BF16).reshape(2048, 512)]
    all_to_all x3 -> x2, waiting for transfers between devices: 58.8 us -> 61.8 us  [the longest x1 33.3 us: on_device(): lax.all_to_all(outgoing.reshape(128, 9, 2, 128), ROWS, 0, 0, tiled=True)]
    reshape x2 -> x1, local copies, waits for them, and re-layouts: 2.84 us -> 0.32 us  [on_device(): section_two = section_two.reshape(512, 512)]
    transpose x2 -> x0, local copies, waits for them, and re-layouts: 2.41 us -> none  [the longest x1 2.28 us: on_device(): section_two.transpose(1, 0, 2)]
    all_to_all x1, waiting for transfers between devices: 5.11 us -> 7.1 us  [on_device(): cells = lax.all_to_all(sent, GROUP, 0, 0, tiled=True)]
  transfers between devices with their start and end apart: 4 -> 3, of which waited for: 4 -> 3; matrix products, arithmetic and copies ran while one was open for 16% -> 8% of each run, Pallas kernels for 1% -> 0%
where the time goes in v2:
time: 131 us; the launch traced here: 128 us
  waiting for transfers between devices  68.9 us (53%)
  starting transfers between devices  34.2 us (26%)
  Pallas kernels  12.2 us (9%)
  other arithmetic  8.62 us (7%)
  local copies, waits for them, and re-layouts  3.68 us (3%)
    all_to_all x1, waiting for transfers between devices, on_device(): lax.all_to_all(outgoing.reshape(128, 9, 2, 128), ROWS, 0, 0, tiled=True)  33.3 us
    all_to_all x1, waiting for transfers between devices, on_device(): lax.all_to_all(section_two.reshape(128, 16, 128), ROWS, 0, 0, tiled=True)  28.5 us
    all_to_all x1, starting transfers between devices, on_device(): lax.all_to_all(outgoing.reshape(128, 9, 2, 128), ROWS, 0, 0, tiled=True)  20.4 us
    all_to_all x1, starting transfers between devices, on_device(): lax.all_to_all(section_two.reshape(128, 16, 128), ROWS, 0, 0, tiled=True)  8.16 us
    all_to_all x1, waiting for transfers between devices, on_device(): cells = lax.all_to_all(sent, GROUP, 0, 0, tiled=True)  7.1 us
    another operation x4, other arithmetic  6.67 us
    all_to_all x1, starting transfers between devices, on_device(): cells = lax.all_to_all(sent, GROUP, 0, 0, tiled=True)  5.65 us
    pallas_call x1, Pallas kernels, on_device(): pl.pallas_call(scatter_body, in_specs=[VMEM], out_specs=VMEM, out_shape=j...  5.18 us
  transfers between devices with their start and end apart: 3, of which 3 were waited for; matrix products, arithmetic and copies ran while one was open for 8% of the time, Pallas kernels for 0%

profile of v2, /device:TPU:1, one launch (start us, length us, event | category | flops | bytes accessed | tf_op | source)
XLA Modules:
  0.0 128.3 jit_solution(6110981788060404944)
XLA Ops:
  0.0 3.9 %shard_map.46 = bf16[2304,128]{1,0:T(8,128)(2,1)} custom-call(bf16[64,64,64]{2,1,0:T(8,128)(2,1)} %tiles_ref.1, s32[1,64]{1,0:T(1,128)} %bitcast.13, s32[1,64]{1,0:T(1,128)} %bitcast.14), custom_call_target="tpu_custom_call" | custom-call | tf_op jit(solution)/shard_map/pallas_call | solution.py:138
  3.9 20.4 %all-to-all-start = ((bf16[128,9,2,128]{3,2,1,0:T(2,128)(2,1)}), bf16[128,9,2,128]{3,2,1,0:T(2,128)(2,1)S(1)}, u32[]{:S(2)}, u32[]{:S(2)}) async-start(bf16[128,9,2,128]{3,2,1,0:T(2,128)(2,1)} %bitcast.11), calls=%async_computation | async-start | bytes 1179648 | tf_op jit(solution)/shard_map/all_to_all | solution.py:145
  24.3 0.1 fusion.65
  24.4 0.1 fusion.67
  24.4 0.1 fusion.69
  24.5 0.1 fusion.54
  24.6 33.3 %all-to-all-done = bf16[128,9,2,128]{3,2,1,0:T(2,128)(2,1)S(1)} async-done(((bf16[128,9,2,128]{3,2,1,0:T(2,128)(2,1)}), bf16[128,9,2,128]{3,2,1,0:T(2,128)(2,1)S(1)}, u32[]{:S(2)}, u32[]{:S(2)}) %all-to-all-start) | async-done | bytes 589856 | tf_op jit(solution)/shard_map/all_to_all | solution.py:145
  57.9 5.2 %shard_map.47 = bf16[8,128,512]{2,1,0:T(8,128)(2,1)} custom-call(bf16[2304,128]{1,0:T(8,128)(2,1)S(1)} %bitcast.10), custom_call_target="tpu_custom_call" | custom-call | tf_op jit(solution)/shard_map/pallas_call | solution.py:146
  63.1 5.6 %all-to-all-start.1 = ((bf16[8,128,512]{2,1,0:T(8,128)(2,1)}), bf16[8,128,512]{2,1,0:T(8,128)(2,1)S(1)}, u32[]{:S(2)}, u32[]{:S(2)}) async-start(bf16[8,128,512]{2,1,0:T(8,128)(2,1)} %shard_map.47), calls=%async_computation.1 | async-start | bytes 2097152 | tf_op jit(solution)/shard_map/all_to_all | solution.py:158
  68.8 0.7 pad_maximum_fusion.4.mix_ref
  69.4 0.7 copy.17.phase_ref
  70.2 0.6 pad_maximum_fusion.2.turn_ref
  70.7 0.3 fusion.24
  71.0 0.3 negate_convert_fusion.2
  71.3 5.0 %negate_convert_fusion = (bf16[512,512]{1,0:T(8,128)(2,1)S(1)}, bf16[512,512]{1,0:T(8,128)(2,1)S(1)}, bf16[512,512]{1,0:T(8,128)(2,1)S(1)}) fusion(s32[512]{0:T(512)S(1)} %fusion.37), kind=kLoop, calls=%fused_computation.8 | loop fusion | flops 5242880 | bytes 1574912 | tf_op jit(solution)/shard_map/convert.11
  76.3 0.3 maximum_maximum_fusion.row_table_ref
  76.6 7.1 %all-to-all-done.1.cells_ref = bf16[8,128,512]{2,1,0:T(8,128)(2,1)S(1)} async-done(((bf16[8,128,512]{2,1,0:T(8,128)(2,1)}), bf16[8,128,512]{2,1,0:T(8,128)(2,1)S(1)}, u32[]{:S(2)}, u32[]{:S(2)}) %all-to-all-start.1) | async-done | bytes 1048608 | tf_op jit(solution)/shard_map/all_to_all | solution.py:158
  83.7 3.2 %shard_map.48 = bf16[2048,128]{1,0:T(8,128)(2,1)} custom-call(f32[8]{0:T(128)} %pad_maximum_fusion.4.mix_ref, bf16[8,128,512]{2,1,0:T(8,128)(2,1)S(1)} %all-to-all-done.1.cells_ref, f32[2,512]{1,0:T(2,128)} %pad_maximum_fusion.2.turn_ref, bf16[1024,1024]{1,0:T(8,128)(2,1)S(1)} %maximum_maximum_fusion.row_table_ref, ...), custom_call_target="tpu_custom_call" | custom-call | tf_op jit(solution)/shard_map/pallas_call | solution.py:181
  86.9 8.2 %all-to-all-start.2 = ((bf16[128,16,128]{2,1,0:T(8,128)(2,1)}), bf16[128,16,128]{2,1,0:T(8,128)(2,1)S(1)}, u32[]{:S(2)}, u32[]{:S(2)}) async-start(bf16[128,16,128]{2,1,0:T(8,128)(2,1)} %bitcast.12), calls=%async_computation.2 | async-start | bytes 1048576 | tf_op jit(solution)/shard_map/all_to_all | solution.py:195
  95.1 1.2 fusion.16
  96.3 0.2 copy.13
  96.5 0.1 stack.34
  96.6 0.1 copy.15
  96.7 0.2 copy.14
  96.9 0.1 stack.36
  97.0 0.1 copy.16
  97.2 0.0 copy-done
  97.2 0.1 convert_element_type.101
  97.2 28.5 %all-to-all-done.2 = bf16[128,16,128]{2,1,0:T(8,128)(2,1)S(1)} async-done(((bf16[128,16,128]{2,1,0:T(8,128)(2,1)}), bf16[128,16,128]{2,1,0:T(8,128)(2,1)S(1)}, u32[]{:S(2)}, u32[]{:S(2)}) %all-to-all-start.2) | async-done | bytes 524320 | tf_op jit(solution)/shard_map/all_to_all | solution.py:195
  125.7 0.3 reshape.514
  126.0 0.4 convolution_multiply_fusion
  126.5 1.8 %copy.18 = f32[256,2,512]{2,1,0:T(2,128)} copy(f32[256,2,512]{2,0,1:T(8,128)S(1)} %convolution_multiply_fusion) | data formatting | bytes 2097152 | tf_op jit(solution)/shard_map/mul | solution.py:207
  (6 shorter events, 0.1 us)
Async XLA Ops:
  3.9 54.0 %all-to-all-start = ((bf16[128,9,2,128]{3,2,1,0:T(2,128)(2,1)}), bf16[128,9,2,128]{3,2,1,0:T(2,128)(2,1)S(1)}, u32[]{:S(2)}, u32[]{:S(2)}) async-start(bf16[128,9,2,128]{3,2,1,0:T(2,128)(2,1)} %bitcast.11), calls=%async_computation | async-start | bytes 1179648 | tf_op jit(solution)/shard_map/all_to_all | solution.py:145
  63.1 20.6 %all-to-all-start.1 = ((bf16[8,128,512]{2,1,0:T(8,128)(2,1)}), bf16[8,128,512]{2,1,0:T(8,128)(2,1)S(1)}, u32[]{:S(2)}, u32[]{:S(2)}) async-start(bf16[8,128,512]{2,1,0:T(8,128)(2,1)} %shard_map.47), calls=%async_computation.1 | async-start | bytes 2097152 | tf_op jit(solution)/shard_map/all_to_all | solution.py:158
  86.9 38.8 %all-to-all-start.2 = ((bf16[128,16,128]{2,1,0:T(8,128)(2,1)}), bf16[128,16,128]{2,1,0:T(8,128)(2,1)S(1)}, u32[]{:S(2)}, u32[]{:S(2)}) async-start(bf16[128,16,128]{2,1,0:T(8,128)(2,1)} %bitcast.12), calls=%async_computation.2 | async-start | bytes 1048576 | tf_op jit(solution)/shard_map/all_to_all | solution.py:195
  96.2 1.0 copy-start

commit v3 on v2

--- a/solution.py
+++ b/solution.py
@@ -29,25 +29,29 @@
 
 
 def pack_body(tiles_ref, dest_ref, place_ref, out_ref, flat_ref, packed_ref):
-    for part in range(4):
-        flat_ref[1024 * part : 1024 * part + 1024, :64] = (
-            tiles_ref[16 * part : 16 * part + 16].reshape(1024, 64).astype(F32)
-        )
+    for tile in range(32):
+        start = 64 * tile
+        flat_ref[start : start + 64, :64] = tiles_ref[tile].astype(F32)
+        flat_ref[start : start + 64, 64:] = tiles_ref[tile + 32].astype(F32)
     place = place_ref[...]
-    labels = jnp.concatenate([place // 16 * 128 + dest_ref[...], place % 16], 1)
-    labels = jnp.broadcast_to(labels.astype(F32), (2, 128))
-    group = lane_group((16, 128))
+    labels = jnp.concatenate([place // 16 * 128 + dest_ref[...], place % 16], 1).astype(F32)
+    group = lax.broadcasted_iota(jnp.int32, (1, 128), 1) // 16
+    swapped = jnp.where(
+        group % 2 == 0, pltpu.roll(labels, 112, 1), pltpu.roll(labels, 16, 1)
+    )
+    labels = [jnp.broadcast_to(row, (2, 128)) for row in (labels, swapped)]
+    odd = lane_group((16, 128)) % 2 == 1
     for chip in range(64):
-        parts = [flat_ref[pl.ds(1024 * g + chip, 16, stride=64), :] for g in range(4)]
+        first = flat_ref[pl.ds(chip, 16, stride=64), :]
+        second = flat_ref[pl.ds(1024 + chip, 16, stride=64), :]
+        values = [
+            jnp.where(odd, pltpu.roll(second, 32, 1), first),
+            jnp.where(odd, first, pltpu.roll(second, 96, 1)),
+        ]
         for core in range(2):
-            value = None
-            for g in range(4):
-                shift = 32 * (g - core) % 128
-                moved = pltpu.roll(parts[g], shift, 1) if shift else parts[g]
-                value = moved if value is None else jnp.where(group == g, moved, value)
             start = 18 * (2 * chip + core)
-            packed_ref[start : start + 16] = value
-            packed_ref[start + 16 : start + 18] = labels
+            packed_ref[start : start + 16] = values[core]
+            packed_ref[start + 16 : start + 18] = labels[core]
     out_ref[...] = packed_ref[...].astype(BF16)
 
 
@@ -125,8 +129,35 @@
     out_ref[...] = flat_ref[...].astype(BF16)
 
 
+def final_body(rows_ref, table_ref, psf_ref, out_ref, flat_ref, values_ref, result_ref, sems):
+    flat_ref[...] = rows_ref[...].astype(F32)
+    for v in range(4):
+        values_ref[:, 128 * v : 128 * v + 128] = flat_ref[pl.ds(v, 512, stride=4), :].astype(BF16)
+    copies = []
+    for part in range(4):
+        start = 64 * part
+        result = jnp.dot(
+            table_ref[128 * part : 128 * part + 128, :],
+            values_ref[...],
+            preferred_element_type=F32,
+        )
+        psf = psf_ref[start : start + 64, :].astype(F32)
+        result_ref[start : start + 64, 0, :] = result[:64] * psf
+        result_ref[start : start + 64, 1, :] = result[64:] * psf
+        window = pl.ds(start, 64)
+        copy = pltpu.make_async_copy(result_ref.at[window], out_ref.at[window], sems.at[part])
+        copy.start()
+        copies.append(copy)
+    for copy in copies:
+        copy.wait()
+
+
 VMEM = pl.BlockSpec(memory_space=pltpu.VMEM)
 SMEM = pl.BlockSpec(memory_space=pltpu.SMEM)
+
+
+def in_vmem(x):
+    return pltpu.with_memory_space_constraint(x, pltpu.VMEM)
 
 
 def on_device(tile_density, tile_dest, tile_place, psf_spectrum):
@@ -140,7 +171,7 @@
         in_specs=[VMEM] * 3,
         out_specs=VMEM,
         out_shape=jax.ShapeDtypeStruct((2304, 128), BF16),
-        scratch_shapes=[pltpu.VMEM((4096, 128), F32), pltpu.VMEM((2304, 128), F32)],
+        scratch_shapes=[pltpu.VMEM((2048, 128), F32), pltpu.VMEM((2304, 128), F32)],
     )(tile_density, tile_dest.reshape(1, 64), tile_place.reshape(1, 64))
     arrived = lax.all_to_all(outgoing.reshape(128, 9, 2, 128), ROWS, 0, 0, tiled=True)
     sent = pl.pallas_call(
@@ -153,10 +184,9 @@
             pltpu.VMEM((2, 512, 512), BF16),
             pltpu.VMEM((2, 256, 512), BF16),
         ],
-    )(pltpu.with_memory_space_constraint(arrived.reshape(2304, 128), pltpu.VMEM))
+    )(in_vmem(arrived.reshape(2304, 128)))
 
     cells = lax.all_to_all(sent, GROUP, 0, 0, tiled=True)
-    cells = pltpu.with_memory_space_constraint(cells, pltpu.VMEM)
 
     order = iota(512)
     column = order % 256 // 32 * 64 + order // 256 * 32 + order % 32
@@ -186,11 +216,11 @@
         scratch_shapes=[pltpu.VMEM((2048, 128), F32)],
     )(
         mix,
-        cells,
-        turn,
-        pltpu.with_memory_space_constraint(row_table, pltpu.VMEM),
-        pltpu.with_memory_space_constraint(slab_table, pltpu.VMEM),
-        phase,
+        in_vmem(cells),
+        in_vmem(turn),
+        in_vmem(row_table),
+        in_vmem(slab_table),
+        in_vmem(phase),
     )
     section_two = lax.all_to_all(section_two.reshape(128, 16, 128), ROWS, 0, 0, tiled=True)
 
@@ -199,12 +229,23 @@
     cosine, sine = table_parts(
         iota(256)[:, None], position[None, :], 256, 1.0 / math.sqrt(32768)
     )
-    final_table = jnp.stack(
-        [jnp.stack([cosine, sine], 2), jnp.stack([-sine, cosine], 2)], 1
-    ).reshape(512, 512).astype(BF16)
-    section_two = section_two.reshape(512, 512)
-    result = jnp.dot(final_table, section_two, preferred_element_type=F32)
-    return result.reshape(256, 2, 512) * psf_spectrum.astype(F32)[:, None, :]
+    real = jnp.stack([cosine, sine], 2).reshape(4, 1, 64, 512)
+    imag = jnp.stack([-sine, cosine], 2).reshape(4, 1, 64, 512)
+    final_table = jnp.concatenate([real, imag], 1).reshape(512, 512).astype(BF16)
+    return pl.pallas_call(
+        final_body,
+        in_specs=[VMEM] * 3,
+        out_specs=pl.BlockSpec(memory_space=pl.ANY),
+        out_shape=jax.ShapeDtypeStruct((256, 2, 512), F32),
+        scratch_shapes=[
+            pltpu.VMEM((2048, 128), F32),
+            pltpu.VMEM((512, 512), BF16),
+            pltpu.VMEM((256, 2, 512), F32),
+            pltpu.SemaphoreType.DMA((4,)),
+        ],
+    )(
+        in_vmem(section_two.reshape(2048, 128)), in_vmem(final_table), in_vmem(psf_spectrum)
+    )
 
 
 def solution(mesh):

time: 131 us -> 129 us (0.985)
  local copies, waits for them, and re-layouts: 3.68 us -> 1.79 us
    mul x1 -> x0, local copies, waits for them, and re-layouts: 1.78 us -> none  [on_device(): return result.reshape(256, 2, 512) * psf_spectrum.astype(F32)[:, None, :]]
    all_to_all x1, waiting for transfers between devices: 28.5 us -> 26.8 us  [on_device(): lax.all_to_all(section_two.reshape(128, 16, 128), ROWS, 0, 0, tiled=True)]
    pallas_call x0 -> x1, Pallas kernels: none -> 1.43 us  [on_device(): pl.pallas_call(final_body, in_specs=[VMEM] * 3, out_specs=pl.BlockSpec(me...]
where the time goes in v3:
time: 129 us; the launch traced here: 126 us
  waiting for transfers between devices  68.6 us (53%)
  starting transfers between devices  34.2 us (27%)
  Pallas kernels  12.6 us (10%)
  other arithmetic  8.76 us (7%)
  local copies, waits for them, and re-layouts  1.79 us (1%)
    all_to_all x1, waiting for transfers between devices, on_device(): lax.all_to_all(outgoing.reshape(128, 9, 2, 128), ROWS, 0, 0, tiled=True)  33.3 us
    all_to_all x1, waiting for transfers between devices, on_device(): lax.all_to_all(section_two.reshape(128, 16, 128), ROWS, 0, 0, tiled=True)  26.8 us
    all_to_all x1, starting transfers between devices, on_device(): lax.all_to_all(outgoing.reshape(128, 9, 2, 128), ROWS, 0, 0, tiled=True)  20.4 us
    all_to_all x1, waiting for transfers between devices, on_device(): cells = lax.all_to_all(sent, GROUP, 0, 0, tiled=True)  8.4 us
    all_to_all x1, starting transfers between devices, on_device(): lax.all_to_all(section_two.reshape(128, 16, 128), ROWS, 0, 0, tiled=True)  8.16 us
    another operation x4, other arithmetic  6.67 us
    all_to_all x1, starting transfers between devices, on_device(): cells = lax.all_to_all(sent, GROUP, 0, 0, tiled=True)  5.66 us
    pallas_call x1, Pallas kernels, on_device(): pl.pallas_call(scatter_body, in_specs=[VMEM], out_specs=VMEM, out_shape=j...  5.18 us
  transfers between devices with their start and end apart: 3, of which 3 were waited for; matrix products, arithmetic and copies ran while one was open for 8% of the time, Pallas kernels for 0%

profile of v3, /device:TPU:1, one launch (start us, length us, event | category | flops | bytes accessed | tf_op | source)
XLA Modules:
  0.0 126.3 jit_solution(17181874383808150044)
XLA Ops:
  0.0 3.0 %shard_map.46 = bf16[2304,128]{1,0:T(8,128)(2,1)} custom-call(bf16[64,64,64]{2,1,0:T(8,128)(2,1)} %tiles_ref.1, s32[1,64]{1,0:T(1,128)} %bitcast.16, s32[1,64]{1,0:T(1,128)} %bitcast.17), custom_call_target="tpu_custom_call" | custom-call | tf_op jit(solution)/shard_map/pallas_call | solution.py:169
  3.0 20.4 %all-to-all-start = ((bf16[128,9,2,128]{3,2,1,0:T(2,128)(2,1)}), bf16[128,9,2,128]{3,2,1,0:T(2,128)(2,1)S(1)}, u32[]{:S(2)}, u32[]{:S(2)}) async-start(bf16[128,9,2,128]{3,2,1,0:T(2,128)(2,1)} %bitcast.14), calls=%async_computation | async-start | bytes 1179648 | tf_op jit(solution)/shard_map/all_to_all | solution.py:176
  23.4 0.1 fusion.62
  23.5 0.1 fusion.64
  23.5 0.1 fusion.66
  23.6 0.1 fusion.51
  23.7 33.3 %all-to-all-done = bf16[128,9,2,128]{3,2,1,0:T(2,128)(2,1)S(1)} async-done(((bf16[128,9,2,128]{3,2,1,0:T(2,128)(2,1)}), bf16[128,9,2,128]{3,2,1,0:T(2,128)(2,1)S(1)}, u32[]{:S(2)}, u32[]{:S(2)}) %all-to-all-start) | async-done | bytes 589856 | tf_op jit(solution)/shard_map/all_to_all | solution.py:176
  57.0 5.2 %shard_map.47 = bf16[8,128,512]{2,1,0:T(8,128)(2,1)} custom-call(bf16[2304,128]{1,0:T(8,128)(2,1)S(1)} %bitcast.11), custom_call_target="tpu_custom_call" | custom-call | tf_op jit(solution)/shard_map/pallas_call | solution.py:177
  62.2 5.7 %all-to-all-start.1 = ((bf16[8,128,512]{2,1,0:T(8,128)(2,1)}), bf16[8,128,512]{2,1,0:T(8,128)(2,1)S(1)}, u32[]{:S(2)}, u32[]{:S(2)}) async-start(bf16[8,128,512]{2,1,0:T(8,128)(2,1)} %shard_map.47), calls=%async_computation.1 | async-start | bytes 2097152 | tf_op jit(solution)/shard_map/all_to_all | solution.py:189
  67.9 0.6 pad_maximum_fusion.5.mix_ref
  68.5 0.1 copy.8.phase_ref
  68.6 0.3 fusion.21
  68.9 0.3 negate_convert_fusion.2
  69.2 5.0 %negate_convert_fusion = (bf16[512,512]{1,0:T(8,128)(2,1)S(1)}, bf16[512,512]{1,0:T(8,128)(2,1)S(1)}, bf16[512,512]{1,0:T(8,128)(2,1)S(1)}) fusion(s32[512]{0:T(512)S(1)} %fusion.34), kind=kLoop, calls=%fused_computation.8 | loop fusion | flops 5242880 | bytes 1574912 | tf_op jit(solution)/shard_map/convert.19
  74.2 0.3 maximum_maximum_fusion.row_table_ref
  74.4 8.4 %all-to-all-done.1.cells_ref = bf16[8,128,512]{2,1,0:T(8,128)(2,1)S(1)} async-done(((bf16[8,128,512]{2,1,0:T(8,128)(2,1)}), bf16[8,128,512]{2,1,0:T(8,128)(2,1)S(1)}, u32[]{:S(2)}, u32[]{:S(2)}) %all-to-all-start.1) | async-done | bytes 1048608 | tf_op jit(solution)/shard_map/all_to_all | solution.py:189
  82.8 3.0 %shard_map.48 = bf16[2048,128]{1,0:T(8,128)(2,1)} custom-call(f32[8]{0:T(128)} %pad_maximum_fusion.5.mix_ref, bf16[8,128,512]{2,1,0:T(8,128)(2,1)S(1)} %all-to-all-done.1.cells_ref, f32[2,512]{1,0:T(2,128)S(1)} %pad_maximum_fusion.3.turn_ref, bf16[1024,1024]{1,0:T(8,128)(2,1)S(1)} %maximum_maximum_fusion.row_table_ref, ...), custom_call_target="tpu_custom_call" | custom-call | tf_op jit(solution)/shard_map/pallas_call | solution.py:211
  85.8 8.2 %all-to-all-start.2 = ((bf16[128,16,128]{2,1,0:T(8,128)(2,1)}), bf16[128,16,128]{2,1,0:T(8,128)(2,1)S(1)}, u32[]{:S(2)}, u32[]{:S(2)}) async-start(bf16[128,16,128]{2,1,0:T(8,128)(2,1)} %bitcast.15), calls=%async_computation.2 | async-start | bytes 1048576 | tf_op jit(solution)/shard_map/all_to_all | solution.py:225
  94.0 1.2 fusion.13
  95.2 0.2 copy.9
  95.4 0.3 reshape.513
  95.7 0.2 copy.10
  95.9 0.0 copy-start
  95.9 0.3 reshape.514
  96.3 0.9 pad_maximum_fusion
  97.2 0.6 copy.11
  97.8 26.8 %all-to-all-done.2 = bf16[128,16,128]{2,1,0:T(8,128)(2,1)S(1)} async-done(((bf16[128,16,128]{2,1,0:T(8,128)(2,1)}), bf16[128,16,128]{2,1,0:T(8,128)(2,1)S(1)}, u32[]{:S(2)}, u32[]{:S(2)}) %all-to-all-start.2) | async-done | bytes 524320 | tf_op jit(solution)/shard_map/all_to_all | solution.py:225
  124.7 0.0 copy-done
  124.7 1.4 %shard_map.49 = f32[256,2,512]{2,1,0:T(2,128)} custom-call(bf16[2048,128]{1,0:T(8,128)(2,1)S(1)} %bitcast.13, bf16[512,512]{1,0:T(8,128)(2,1)S(1)} %bitcast.12, bf16[256,512]{1,0:T(8,128)(2,1)S(1)} %copy-done), custom_call_target="tpu_custom_call" | custom-call | tf_op jit(solution)/shard_map/pallas_call | solution.py:235
  (6 shorter events, 0.1 us)
Async XLA Ops:
  3.0 54.0 %all-to-all-start = ((bf16[128,9,2,128]{3,2,1,0:T(2,128)(2,1)}), bf16[128,9,2,128]{3,2,1,0:T(2,128)(2,1)S(1)}, u32[]{:S(2)}, u32[]{:S(2)}) async-start(bf16[128,9,2,128]{3,2,1,0:T(2,128)(2,1)} %bitcast.14), calls=%async_computation | async-start | bytes 1179648 | tf_op jit(solution)/shard_map/all_to_all | solution.py:176
  62.2 20.6 %all-to-all-start.1 = ((bf16[8,128,512]{2,1,0:T(8,128)(2,1)}), bf16[8,128,512]{2,1,0:T(8,128)(2,1)S(1)}, u32[]{:S(2)}, u32[]{:S(2)}) async-start(bf16[8,128,512]{2,1,0:T(8,128)(2,1)} %shard_map.47), calls=%async_computation.1 | async-start | bytes 2097152 | tf_op jit(solution)/shard_map/all_to_all | solution.py:189
  85.8 38.8 %all-to-all-start.2 = ((bf16[128,16,128]{2,1,0:T(8,128)(2,1)}), bf16[128,16,128]{2,1,0:T(8,128)(2,1)S(1)}, u32[]{:S(2)}, u32[]{:S(2)}) async-start(bf16[128,16,128]{2,1,0:T(8,128)(2,1)} %bitcast.15), calls=%async_computation.2 | async-start | bytes 1048576 | tf_op jit(solution)/shard_map/all_to_all | solution.py:225
  95.9 28.7 %copy-start = (bf16[256,512]{1,0:T(8,128)(2,1)S(1)}, bf16[256,512]{1,0:T(8,128)(2,1)}, u32[]{:S(2)}) copy-start(bf16[256,512]{1,0:T(8,128)(2,1)} %psf_ref.1) | copy-start | bytes 786436

commit v4 on v3

v4 whole, which is shorter than its diff:
```python
import math

import jax
import jax.numpy as jnp
from jax import lax
from jax.experimental import pallas as pl
from jax.experimental.pallas import tpu as pltpu
from jax.sharding import Mesh
from jax.sharding import PartitionSpec as P

ROWS = ("chip", "core")
EVERYWHERE = ("chip", "core", "cols")
F32 = jnp.float32
BF16 = jnp.bfloat16


def cosines(index, period):
    return jnp.cos(2.0 * math.pi / period * (index % period).astype(F32))


def lane_group(shape):
    return lax.broadcasted_iota(jnp.int32, shape, 1) // 32


def pack_body(tiles_ref, dest_ref, place_ref, out_ref, flat_ref, packed_ref):
    for tile in range(32):
        start = 64 * tile
        flat_ref[start : start + 64, :64] = tiles_ref[tile].astype(F32)
        flat_ref[start : start + 64, 64:] = tiles_ref[tile + 32].astype(F32)
    place = place_ref[...]
    labels = jnp.concatenate([place // 16 * 128 + dest_ref[...], place % 16], 1).astype(F32)
    group = lax.broadcasted_iota(jnp.int32, (1, 128), 1) // 16
    swapped = jnp.where(
        group % 2 == 0, pltpu.roll(labels, 112, 1), pltpu.roll(labels, 16, 1)
    )
    labels = [jnp.broadcast_to(row, (2, 128)) for row in (labels, swapped)]
    odd = lane_group((16, 128)) % 2 == 1
    for chip in range(64):
        first = flat_ref[pl.ds(chip, 16, stride=64), :]
        second = flat_ref[pl.ds(1024 + chip, 16, stride=64), :]
        values = [
            jnp.where(odd, pltpu.roll(second, 32, 1), first),
            jnp.where(odd, first, pltpu.roll(second, 96, 1)),
        ]
        for core in range(2):
            start = 18 * (2 * chip + core)
            packed_ref[start : start + 16] = values[core]
            packed_ref[start + 16 : start + 18] = labels[core]
    out_ref[...] = packed_ref[...].astype(BF16)


def scatter_body(tiles_ref, order_ref, out_ref, flat_ref, spread_ref, hot_ref):
    flat_ref[...] = tiles_ref[...].astype(F32)
    labels = flat_ref[pl.ds(16, 128, stride=18), :]
    named = jnp.transpose(labels)
    group = lane_group((128, 128))
    lane = group.astype(F32)
    slab = lax.broadcasted_iota(jnp.int32, (256, 128), 0).astype(F32)
    total = None
    for step in range(16):
        slot = step % 2
        values = flat_ref[pl.ds(step, 128, stride=18), :]
        rolls = [values] + [pltpu.roll(values, 32 * j, 1) for j in range(1, 4)]
        for g in range(4):
            copies = rolls[(-g) % 4]
            for h in range(1, 4):
                copies = jnp.where(group == h, rolls[(h - g) % 4], copies)
            copies = copies.astype(BF16)
            tile = 16 * g + step
            place = jnp.broadcast_to(labels[:, 64 + tile : 65 + tile], (128, 128)) - lane
            place = place.astype(BF16)
            for m in range(4):
                spread_ref[slot, 128 * g : 128 * g + 128, 128 * m : 128 * m + 128] = jnp.where(
                    place == jnp.array(4.0 * m, BF16), copies, jnp.zeros_like(copies)
                )
            hot = jnp.broadcast_to(named[tile : tile + 1, :], (256, 128)) == slab
            hot_ref[slot, :, 128 * g : 128 * g + 128] = jnp.where(hot, 1.0, 0.0).astype(BF16)
        part = jnp.dot(hot_ref[slot], spread_ref[slot], preferred_element_type=F32)
        total = part if total is None else total + part
    total = jnp.dot(total.astype(BF16), order_ref[...], preferred_element_type=F32)
    for octet in range(4):
        out_ref[octet] = total[:, 128 * octet : 128 * octet + 128].astype(BF16)


def turned(first, second, sign):
    return first + sign * pltpu.roll(second, 64, 1)


def lane_sign(shape):
    lane = lax.broadcasted_iota(jnp.int32, shape, 1)
    return jnp.where(lane < 64, 1.0, -1.0)


def rows_body(cells_ref, mix_table_ref, slab_table_ref, phase_ref, out_ref, flat_ref):
    cells = jnp.concatenate([cells_ref[e] for e in range(4)], 1)
    spectrum = jnp.dot(cells, mix_table_ref[...], preferred_element_type=F32).astype(BF16)
    sign = lane_sign((128, 128))
    for r in range(4):
        start = 128 * (r // 2)
        values = spectrum[start : start + 128, 512 * (r % 2) : 512 * (r % 2) + 512]
        both = jnp.dot(slab_table_ref[...], values, preferred_element_type=F32)
        first, second = both[:128], both[128:]
        cosine, sine = phase_ref[:, r : r + 1], phase_ref[:, 4 + r : 5 + r]
        straight = first * cosine - second * sine
        crossed = second * cosine + first * sine
        for k in range(4):
            lanes = slice(128 * k, 128 * k + 128)
            flat_ref[pl.ds(4 * k + r, 128, stride=16), :] = turned(
                straight[:, lanes], crossed[:, lanes], sign
            )
    out_ref[...] = flat_ref[...].astype(BF16)


def final_body(
    rows_ref,
    table_ref,
    cell_table_hbm,
    psf_ref,
    out_ref,
    flat_ref,
    values_ref,
    cell_table_ref,
    result_ref,
    sems,
):
    fetch = pltpu.make_async_copy(cell_table_hbm, cell_table_ref, sems.at[2])
    fetch.start()
    flat_ref[...] = rows_ref[...].astype(F32)
    for h in range(8):
        for r in range(4):
            values_ref[64 * r : 64 * r + 64, 128 * h : 128 * h + 128] = flat_ref[
                pl.ds(4 * h + r, 64, stride=32), :
            ].astype(BF16)
    both = jnp.dot(table_ref[...], values_ref[...], preferred_element_type=F32)
    sign = lane_sign((256, 128))
    for h in range(8):
        lanes = slice(128 * h, 128 * h + 128)
        values_ref[:, lanes] = turned(both[:256, lanes], both[256:, lanes], sign).astype(BF16)
    fetch.wait()
    copies = []
    for part in range(2):
        window = pl.ds(128 * part, 128)
        result = jnp.dot(
            values_ref[window, :], cell_table_ref[...], preferred_element_type=F32
        )
        psf = psf_ref[window, :].astype(F32)
        result_ref[window, 0, :] = result[:, :512] * psf
        result_ref[window, 1, :] = result[:, 512:] * psf
        copy = pltpu.make_async_copy(result_ref.at[window], out_ref.at[window], sems.at[part])
        copy.start()
        copies.append(copy)
    for copy in copies:
        copy.wait()


VMEM = pl.BlockSpec(memory_space=pltpu.VMEM)


def in_vmem(x):
    return pltpu.with_memory_space_constraint(x, pltpu.VMEM)


def on_device(tile_density, tile_dest, tile_place, psf_spectrum):
    chip = lax.axis_index("chip")
    core = lax.axis_index("core")
    me_col = lax.axis_index("cols")
    iota = lambda n: jnp.arange(n, dtype=jnp.int32)

    member = 4 * core + me_col

    out = iota(512)
    source = out % 128 // 8 * 32 + out // 128 * 8 + out % 8
    order_table = (iota(512)[:, None] == source[None, :]).astype(BF16)

    given, out = iota(512)[:, None], iota(1024)[None, :]
    column = given // 128 * 512 + given % 64 // 8 * 64 + 8 * member + given % 8
    frequency = out % 512 // 128 + 4 * (out % 64 // 8)
    same = (given % 128 // 64 == out // 512) & (given % 8 == out % 8)
    mix_table = cosines(column * frequency + 512 * (out % 128 // 64), 2048)
    mix_table = jnp.where(same, mix_table * (1.0 / math.sqrt(2048)), 0.0).astype(BF16)

    given, out = iota(128)[None, :], iota(256)[:, None]
    slab_table = cosines(given * (out % 128) + 96 * (out // 128), 128).astype(BF16)
    part = iota(8)[None, :]
    phase = cosines(
        (64 * (part % 4) + chip) * iota(128)[:, None] + 24576 * (part // 4), 32768
    )

    given, out = iota(256)[None, :], iota(512)[:, None]
    final_table = cosines(given * (out % 256) + 192 * (out // 256), 256)
    final_table = (final_table * (1.0 / math.sqrt(32768))).astype(BF16)

    given, out = iota(1024)[:, None], iota(1024)[None, :]
    cell = given // 128 * 8 + given % 8
    turn = 16 * (out // 512 - given % 128 // 64)
    cell_table = cosines(cell * (out % 512 // 8) + turn + 64, 64)
    cell_table = jnp.where(given % 64 // 8 == out % 8, cell_table, 0.0).astype(BF16)

    outgoing = pl.pallas_call(
        pack_body,
        in_specs=[VMEM] * 3,
        out_specs=VMEM,
        out_shape=jax.ShapeDtypeStruct((2304, 128), BF16),
        scratch_shapes=[pltpu.VMEM((2048, 128), F32), pltpu.VMEM((2304, 128), F32)],
    )(tile_density, tile_dest.reshape(1, 64), tile_place.reshape(1, 64))
    arrived = lax.all_to_all(outgoing.reshape(128, 9, 2, 128), ROWS, 0, 0, tiled=True)
    arrived, order_table, mix_table, slab_table, phase, final_table, cell_table = (
        lax.optimization_barrier(
            (arrived, order_table, mix_table, slab_table, phase, final_table, cell_table)
        )
    )
    sent = pl.pallas_call(
        scatter_body,
        in_specs=[VMEM] * 2,
        out_specs=VMEM,
        out_shape=jax.ShapeDtypeStruct((4, 256, 128), BF16),
        scratch_shapes=[
            pltpu.VMEM((2304, 128), F32),
            pltpu.VMEM((2, 512, 512), BF16),
            pltpu.VMEM((2, 256, 512), BF16),
        ],
    )(in_vmem(arrived.reshape(2304, 128)), in_vmem(order_table))

    cells = lax.all_to_all(sent, "cols", 0, 0, tiled=True)
    section_two = pl.pallas_call(
        rows_body,
        in_specs=[VMEM] * 4,
        out_specs=VMEM,
        out_shape=jax.ShapeDtypeStruct((2048, 128), BF16),
        scratch_shapes=[pltpu.VMEM((2048, 128), F32)],
    )(in_vmem(cells), in_vmem(mix_table), in_vmem(slab_table), in_vmem(phase))

    section_two = lax.all_to_all(
        section_two.reshape(512, 2, 2, 128), EVERYWHERE, 0, 0, tiled=True
    )
    return pl.pallas_call(
        final_body,
        in_specs=[VMEM, VMEM, pl.BlockSpec(memory_space=pl.ANY), VMEM],
        out_specs=pl.BlockSpec(memory_space=pl.ANY),
        out_shape=jax.ShapeDtypeStruct((256, 2, 512), F32),
        scratch_shapes=[
            pltpu.VMEM((2048, 128), F32),
            pltpu.VMEM((256, 1024), BF16),
            pltpu.VMEM((1024, 1024), BF16),
            pltpu.VMEM((256, 2, 512), F32),
            pltpu.SemaphoreType.DMA((3,)),
        ],
    )(
        in_vmem(section_two.reshape(2048, 128)),
        in_vmem(final_table),
        cell_table,
        in_vmem(psf_spectrum),
    )


def solution(mesh):
    rows, cols = mesh.devices.shape
    split = Mesh(mesh.devices.reshape(rows // 2, 2, cols), EVERYWHERE)
    in_specs = (P(EVERYWHERE, None, None), P(EVERYWHERE, None), P(EVERYWHERE), P(ROWS, "cols"))
    return jax.shard_map(
        on_device,
        mesh=split,
        in_specs=in_specs,
        out_specs=P(ROWS, None, "cols"),
        check_vma=False,
    )
```

time: 129 us -> 132 us (1.023); the launches traced: 126 us -> 131 us
  waiting for transfers between devices: 68.6 us -> 3.35 us
  blocking collectives: 0 us -> 62.4 us
  other arithmetic: 8.76 us -> 30.2 us
  starting transfers between devices: 34.2 us -> 20.4 us
  Pallas kernels: 12.6 us -> 14.6 us
  local copies, waits for them, and re-layouts: 1.79 us -> 0.01 us
    all_to_all x0 -> x2, blocking collectives: none -> 62.4 us  [the longest x1 52.6 us: on_device(): lax.all_to_all(section_two.reshape(512, 2, 2, 128), EVERYWHERE, 0, 0, til...]
    all_to_all x2 -> x0, waiting for transfers between devices: 35.2 us -> none  [the longest x1 26.8 us: on_device(): lax.all_to_all(section_two.reshape(128, 16, 128), ROWS, 0, 0, tiled=True)]
    all_to_all x1, waiting for transfers between devices: 33.3 us -> 3.35 us  [on_device(): lax.all_to_all(outgoing.reshape(128, 9, 2, 128), ROWS, 0, 0, tiled=True)]
    convert_element_type x0 -> x5, other arithmetic: none -> 29.8 us  [the longest x1 18.2 us: on_device(): jnp.where(given % 64 // 8 == out % 8, cell_table, 0.0).astype(BF16)]
    all_to_all x2 -> x0, starting transfers between devices: 13.8 us -> none  [the longest x1 8.16 us: on_device(): lax.all_to_all(section_two.reshape(128, 16, 128), ROWS, 0, 0, tiled=True)]
    another operation x7 -> x0, other arithmetic: 6.73 us -> none
    pallas_call x3, Pallas kernels: 9.59 us -> 11.5 us  [the longest x1 5.11 us: on_device(): pl.pallas_call(scatter_body, in_specs=[VMEM] * 2, out_specs=VMEM, out_sha...]
    concatenate x4 -> x0, other arithmetic: 1.76 us -> none  [the longest x1 0.88 us: on_device(): jnp.concatenate([real, imag], 1).reshape(512, 512).astype(BF16)]
  transfers between devices with their start and end apart: 3 -> 1, of which waited for: 3 -> 1; matrix products, arithmetic and copies ran while one was open for 8% -> 23% of each run, Pallas kernels for 0% -> 0%
where the time goes in v4:
time: 132 us; the launch traced here: 131 us
  blocking collectives  62.4 us (47%)
  other arithmetic  30.2 us (23%)
  starting transfers between devices  20.4 us (15%)
  Pallas kernels  14.6 us (11%)
  waiting for transfers between devices  3.35 us (3%)
    all_to_all x1, blocking collectives, on_device(): lax.all_to_all(section_two.reshape(512, 2, 2, 128), EVERYWHERE, 0, 0, til...  52.6 us
    all_to_all x1, starting transfers between devices, on_device(): lax.all_to_all(outgoing.reshape(128, 9, 2, 128), ROWS, 0, 0, tiled=True)  20.4 us
    convert_element_type x1, other arithmetic, on_device(): jnp.where(given % 64 // 8 == out % 8, cell_table, 0.0).astype(BF16)  18.2 us
    all_to_all x1, blocking collectives, on_device(): cells = lax.all_to_all(sent, 'cols', 0, 0, tiled=True)  9.85 us
    convert_element_type x1, other arithmetic, on_device(): jnp.where(same, mix_table * (1.0 / math.sqrt(2048)), 0.0).astype(BF16)  8.52 us
    pallas_call x1, Pallas kernels, on_device(): pl.pallas_call(scatter_body, in_specs=[VMEM] * 2, out_specs=VMEM, out_sha...  5.11 us
    pallas_call x1, Pallas kernels, on_device(): pl.pallas_call(final_body, in_specs=[VMEM, VMEM, pl.BlockSpec(memory_spac...  4.44 us
    all_to_all x1, waiting for transfers between devices, on_device(): lax.all_to_all(outgoing.reshape(128, 9, 2, 128), ROWS, 0, 0, tiled=True)  3.35 us
  transfers between devices with their start and end apart: 1, of which 1 were waited for; matrix products, arithmetic and copies ran while one was open for 23% of the time, Pallas kernels for 0%

profile of v4, /device:TPU:1, one launch (start us, length us, event | category | flops | bytes accessed | tf_op | source)
XLA Modules:
  0.0 131.2 jit_solution(16829521639497805580)
XLA Ops:
  0.0 3.0 %shard_map.46 = bf16[2304,128]{1,0:T(8,128)(2,1)} custom-call(bf16[64,64,64]{2,1,0:T(8,128)(2,1)} %tiles_ref.1, s32[1,64]{1,0:T(1,128)} %bitcast.10, s32[1,64]{1,0:T(1,128)} %bitcast.11), custom_call_target="tpu_custom_call" | custom-call | tf_op jit(solution)/shard_map/pallas_call | solution.py:199
  3.0 20.4 %all-to-all-start = ((bf16[128,9,2,128]{3,2,1,0:T(2,128)(2,1)}), bf16[128,9,2,128]{3,2,1,0:T(2,128)(2,1)S(1)}, u32[]{:S(2)}, u32[]{:S(2)}) async-start(bf16[128,9,2,128]{3,2,1,0:T(2,128)(2,1)} %bitcast.8), calls=%async_computation | async-start | bytes 1179648 | tf_op jit(solution)/shard_map/all_to_all | solution.py:206
  23.6 0.3 fusion.28.phase_ref
  23.8 0.6 fusion.24.slab_table_ref
  24.4 2.4 %fusion.19.table_ref = bf16[512,256]{1,0:T(8,128)(2,1)S(1)} fusion(s32[512]{0:T(512)S(1)} %get-tuple-element.30, s32[512]{0:T(512)S(1)} %get-tuple-element.29), kind=kLoop, calls=%fused_computation.29 | loop fusion | flops 2228224 | bytes 266240 | tf_op jit(solution)/shard_map/convert_element_type | solution.py:191
  26.8 0.1 fusion.13.order_ref
  27.0 8.5 %fusion.12.mix_table_ref = bf16[512,1024]{1,0:T(8,128)(2,1)S(1)} fusion(s32[1024]{0:T(1024)S(1)} %get-tuple-element.24, s32[1024]{0:T(1024)S(1)} %get-tuple-element.23, s32[512]{0:T(512)S(1)} %fusion.79, s32[1024]{0:T(1024)S(1)} %get-tuple-element.19, s32[1024]{0:T(1024)S(1)} %get-tuple-element.20, s32[512]{0:T(512)S(1)} %get-tuple-element.21, ...), kind=kLoop, calls=%fused_computation.18 | loop fusion | flops 11010048 | bytes 1071104 | tf_op jit(solution)/shard_map/convert_element_type | solution.py:180
  35.5 18.2 %fusion.5.cell_table_hbm = bf16[1024,1024]{1,0:T(8,128)(2,1)} fusion(s32[1024]{0:T(1024)S(1)} %get-tuple-element.32, s32[1024]{0:T(1024)S(1)} %get-tuple-element.20, s32[1024]{0:T(1024)S(1)} %get-tuple-element.31, s32[1024]{0:T(1024)S(1)} %get-tuple-element.34, s32[1024]{0:T(1024)S(1)} %get-tuple-element.19, s32[1024]{0:T(1024)S(1)} %get-tuple-element.33), kind=kLoop, calls=%fused_computation.8 | loop fusion | flops 22020096 | bytes 2121728 | tf_op jit(solution)/shard_map/convert_element_type | solution.py:197
  53.7 3.4 %all-to-all-done = bf16[128,9,2,128]{3,2,1,0:T(2,128)(2,1)S(1)} async-done(((bf16[128,9,2,128]{3,2,1,0:T(2,128)(2,1)}), bf16[128,9,2,128]{3,2,1,0:T(2,128)(2,1)S(1)}, u32[]{:S(2)}, u32[]{:S(2)}) %all-to-all-start) | async-done | bytes 589856 | tf_op jit(solution)/shard_map/all_to_all | solution.py:206
  57.0 5.1 %shard_map.47 = bf16[4,256,128]{2,1,0:T(8,128)(2,1)} custom-call(bf16[2304,128]{1,0:T(8,128)(2,1)S(1)} %bitcast.6, bf16[512,512]{1,0:T(8,128)(2,1)S(1)} %fusion.13.order_ref), custom_call_target="tpu_custom_call" | custom-call | tf_op jit(solution)/shard_map/pallas_call | solution.py:212
  62.2 0.0 copy-start
  62.2 9.8 %all_to_all.15.cells_ref = bf16[4,256,128]{2,1,0:T(8,128)(2,1)S(1)} all-to-all(bf16[4,256,128]{2,1,0:T(8,128)(2,1)} %shard_map.47), channel_id=1, replica_groups=mesh['chip'=64,'core'=2,'cols'=4] {'cols'}, dimensions={0} | all-to-all | bytes 524288 | tf_op jit(solution)/shard_map/all_to_all | solution.py:224
  72.0 2.0 %shard_map.48 = bf16[2048,128]{1,0:T(8,128)(2,1)} custom-call(bf16[4,256,128]{2,1,0:T(8,128)(2,1)S(1)} %all_to_all.15.cells_ref, bf16[512,1024]{1,0:T(8,128)(2,1)S(1)} %fusion.12.mix_table_ref, bf16[256,128]{1,0:T(8,128)(2,1)S(1)} %fusion.24.slab_table_ref, f32[128,8]{1,0:T(8,128)S(1)} %fusion.28.phase_ref), custom_call_target="tpu_custom_call" | custom-call | tf_op jit(solution)/shard_map/pallas_call | solution.py:225
  74.0 52.6 %all_to_all.16 = bf16[512,2,2,128]{3,2,1,0:T(2,128)(2,1)S(1)} all-to-all(bf16[512,2,2,128]{3,2,1,0:T(2,128)(2,1)} %bitcast.9), channel_id=1, replica_groups=mesh['chip'=64,'core'=2,'cols'=4] {'chip','core','cols'}, dimensions={0} | all-to-all | bytes 1048576 | tf_op jit(solution)/shard_map/all_to_all | solution.py:233
  126.6 0.0 copy-done
  126.6 4.4 %shard_map.49 = f32[256,2,512]{2,1,0:T(2,128)} custom-call(bf16[2048,128]{1,0:T(8,128)(2,1)S(1)} %bitcast.7, bf16[512,256]{1,0:T(8,128)(2,1)S(1)} %fusion.19.table_ref, bf16[1024,1024]{1,0:T(8,128)(2,1)} %fusion.5.cell_table_hbm, bf16[256,512]{1,0:T(8,128)(2,1)S(1)} %copy-done), custom_call_target="tpu_custom_call" | custom-call | tf_op jit(solution)/shard_map/pallas_call | solution.py:236
  (10 shorter events, 0.1 us)
Async XLA Ops:
  3.0 54.0 %all-to-all-start = ((bf16[128,9,2,128]{3,2,1,0:T(2,128)(2,1)}), bf16[128,9,2,128]{3,2,1,0:T(2,128)(2,1)S(1)}, u32[]{:S(2)}, u32[]{:S(2)}) async-start(bf16[128,9,2,128]{3,2,1,0:T(2,128)(2,1)} %bitcast.8), calls=%async_computation | async-start | bytes 1179648 | tf_op jit(solution)/shard_map/all_to_all | solution.py:206
  62.2 64.4 %copy-start = (bf16[256,512]{1,0:T(8,128)(2,1)S(1)}, bf16[256,512]{1,0:T(8,128)(2,1)}, u32[]{:S(2)}) copy-start(bf16[256,512]{1,0:T(8,128)(2,1)} %psf_ref.1) | copy-start | bytes 786436

commit v5 on v4

--- a/solution.py
+++ b/solution.py
@@ -82,32 +82,39 @@
         out_ref[octet] = total[:, 128 * octet : 128 * octet + 128].astype(BF16)
 
 
-def turned(first, second, sign):
-    return first + sign * pltpu.roll(second, 64, 1)
-
-
 def lane_sign(shape):
     lane = lax.broadcasted_iota(jnp.int32, shape, 1)
     return jnp.where(lane < 64, 1.0, -1.0)
 
 
 def rows_body(cells_ref, mix_table_ref, slab_table_ref, phase_ref, out_ref, flat_ref):
-    cells = jnp.concatenate([cells_ref[e] for e in range(4)], 1)
-    spectrum = jnp.dot(cells, mix_table_ref[...], preferred_element_type=F32).astype(BF16)
     sign = lane_sign((128, 128))
-    for r in range(4):
-        start = 128 * (r // 2)
-        values = spectrum[start : start + 128, 512 * (r % 2) : 512 * (r % 2) + 512]
-        both = jnp.dot(slab_table_ref[...], values, preferred_element_type=F32)
-        first, second = both[:128], both[128:]
-        cosine, sine = phase_ref[:, r : r + 1], phase_ref[:, 4 + r : 5 + r]
-        straight = first * cosine - second * sine
-        crossed = second * cosine + first * sine
-        for k in range(4):
-            lanes = slice(128 * k, 128 * k + 128)
-            flat_ref[pl.ds(4 * k + r, 128, stride=16), :] = turned(
-                straight[:, lanes], crossed[:, lanes], sign
-            )
+    left = lax.broadcasted_iota(jnp.int32, (256, 128), 1) < 64
+    for low in range(2):
+        pairs = []
+        for e in (0, 2):
+            first, second = cells_ref[e].astype(F32), cells_ref[e + 1].astype(F32)
+            if low == 0:
+                second = pltpu.roll(second, 64, 1)
+            else:
+                first = pltpu.roll(first, 64, 1)
+            pairs.append(jnp.where(left, first, second).astype(BF16))
+        spectrum = jnp.dot(
+            jnp.concatenate(pairs, 1), mix_table_ref[...], preferred_element_type=F32
+        ).astype(BF16)
+        for half in range(2):
+            r = 2 * half + low
+            values = spectrum[128 * half : 128 * half + 128]
+            both = jnp.dot(slab_table_ref[...], values, preferred_element_type=F32)
+            first, second = both[:128], both[128:]
+            cosine, sine = phase_ref[:, r : r + 1], phase_ref[:, 4 + r : 5 + r]
+            straight = first * cosine - second * sine
+            crossed = second * cosine + first * sine
+            for k in range(4):
+                lanes = slice(128 * k, 128 * k + 128)
+                flat_ref[pl.ds(4 * k + r, 128, stride=16), :] = straight[
+                    :, lanes
+                ] + sign * pltpu.roll(crossed[:, lanes], 64, 1)
     out_ref[...] = flat_ref[...].astype(BF16)
 
 
@@ -120,10 +127,11 @@
     flat_ref,
     values_ref,
     cell_table_ref,
+    stacked_ref,
     result_ref,
     sems,
 ):
-    fetch = pltpu.make_async_copy(cell_table_hbm, cell_table_ref, sems.at[2])
+    fetch = pltpu.make_async_copy(cell_table_hbm, cell_table_ref, sems.at[4])
     fetch.start()
     flat_ref[...] = rows_ref[...].astype(F32)
     for h in range(8):
@@ -131,21 +139,21 @@
             values_ref[64 * r : 64 * r + 64, 128 * h : 128 * h + 128] = flat_ref[
                 pl.ds(4 * h + r, 64, stride=32), :
             ].astype(BF16)
-    both = jnp.dot(table_ref[...], values_ref[...], preferred_element_type=F32)
-    sign = lane_sign((256, 128))
-    for h in range(8):
-        lanes = slice(128 * h, 128 * h + 128)
-        values_ref[:, lanes] = turned(both[:256, lanes], both[256:, lanes], sign).astype(BF16)
     fetch.wait()
+    spectrum = jnp.dot(values_ref[...], cell_table_ref[...], preferred_element_type=F32)
+    stacked_ref[:256] = spectrum[:, :512].astype(BF16)
+    stacked_ref[256:] = spectrum[:, 512:].astype(BF16)
     copies = []
-    for part in range(2):
-        window = pl.ds(128 * part, 128)
+    for part in range(4):
+        window = pl.ds(64 * part, 64)
         result = jnp.dot(
-            values_ref[window, :], cell_table_ref[...], preferred_element_type=F32
+            table_ref[128 * part : 128 * part + 128, :],
+            stacked_ref[...],
+            preferred_element_type=F32,
         )
         psf = psf_ref[window, :].astype(F32)
-        result_ref[window, 0, :] = result[:, :512] * psf
-        result_ref[window, 1, :] = result[:, 512:] * psf
+        result_ref[window, 0, :] = result[:64] * psf
+        result_ref[window, 1, :] = result[64:] * psf
         copy = pltpu.make_async_copy(result_ref.at[window], out_ref.at[window], sems.at[part])
         copy.start()
         copies.append(copy)
@@ -172,12 +180,13 @@
     source = out % 128 // 8 * 32 + out // 128 * 8 + out % 8
     order_table = (iota(512)[:, None] == source[None, :]).astype(BF16)
 
-    given, out = iota(512)[:, None], iota(1024)[None, :]
-    column = given // 128 * 512 + given % 64 // 8 * 64 + 8 * member + given % 8
-    frequency = out % 512 // 128 + 4 * (out % 64 // 8)
-    same = (given % 128 // 64 == out // 512) & (given % 8 == out % 8)
+    given, out = iota(256)[:, None], iota(512)[None, :]
+    column = given // 8 * 64 + 8 * member + given % 8
+    frequency = out // 128 + 4 * (out % 64 // 8)
     mix_table = cosines(column * frequency + 512 * (out % 128 // 64), 2048)
-    mix_table = jnp.where(same, mix_table * (1.0 / math.sqrt(2048)), 0.0).astype(BF16)
+    mix_table = jnp.where(
+        given % 8 == out % 8, mix_table * (1.0 / math.sqrt(2048)), 0.0
+    ).astype(BF16)
 
     given, out = iota(128)[None, :], iota(256)[:, None]
     slab_table = cosines(given * (out % 128) + 96 * (out // 128), 128).astype(BF16)
@@ -186,15 +195,21 @@
         (64 * (part % 4) + chip) * iota(128)[:, None] + 24576 * (part // 4), 32768
     )
 
-    given, out = iota(256)[None, :], iota(512)[:, None]
-    final_table = cosines(given * (out % 256) + 192 * (out // 256), 256)
+    given, out = iota(512)[None, :], iota(512)[:, None]
+    frequency = out // 128 * 64 + out % 64
+    turn = 64 * (out % 128 // 64) - 64 * (given // 256) + 256
+    final_table = cosines(given % 256 * frequency + turn, 256)
     final_table = (final_table * (1.0 / math.sqrt(32768))).astype(BF16)
 
+    given, out = iota(128)[:, None], iota(128)[None, :]
+    turn = 16 * (out // 64 - given % 16 // 8) + 64
+    cell_table = cosines((given // 16 * 8 + given % 8) * (out % 64) + turn, 64).astype(BF16)
     given, out = iota(1024)[:, None], iota(1024)[None, :]
-    cell = given // 128 * 8 + given % 8
-    turn = 16 * (out // 512 - given % 128 // 64)
-    cell_table = cosines(cell * (out % 512 // 8) + turn + 64, 64)
-    cell_table = jnp.where(given % 64 // 8 == out % 8, cell_table, 0.0).astype(BF16)
+    from_rows = given // 64 * 8 + given % 8 == iota(128)[None, :]
+    to_columns = iota(128)[:, None] == out // 8
+    cell_table = jnp.dot(from_rows.astype(BF16), cell_table)
+    cell_table = jnp.dot(cell_table, to_columns.astype(BF16))
+    cell_table = jnp.where(given % 64 // 8 == out % 8, cell_table, jnp.zeros_like(cell_table))
 
     outgoing = pl.pallas_call(
         pack_body,
@@ -242,8 +257,9 @@
             pltpu.VMEM((2048, 128), F32),
             pltpu.VMEM((256, 1024), BF16),
             pltpu.VMEM((1024, 1024), BF16),
+            pltpu.VMEM((512, 512), BF16),
             pltpu.VMEM((256, 2, 512), F32),
-            pltpu.SemaphoreType.DMA((3,)),
+            pltpu.SemaphoreType.DMA((5,)),
         ],
     )(
         in_vmem(section_two.reshape(2048, 128)),

time: 132 us -> 126 us (0.955)
  other arithmetic: 30.2 us -> 7.91 us
  waiting for transfers between devices: 3.35 us -> 23.1 us
  blocking collectives: 62.4 us -> 58.3 us
  matrix products: 0 us -> 2.5 us
    convert_element_type x2 -> x1, other arithmetic: 26.7 us -> 2.25 us  [on_device(): mix_table = jnp.where(given % 8 == out % 8, mix_table * (1.0 / math.sqrt(...]
    all_to_all x1, waiting for transfers between devices: 3.35 us -> 23.1 us  [on_device(): lax.all_to_all(outgoing.reshape(128, 9, 2, 128), ROWS, 0, 0, tiled=True)]
    all_to_all x1, blocking collectives: 52.6 us -> 48.6 us  [on_device(): lax.all_to_all(section_two.reshape(512, 2, 2, 128), EVERYWHERE, 0, 0, til...]
    dot_general x0 -> x1, matrix products: none -> 2.5 us  [on_device(): cell_table = jnp.dot(cell_table, to_columns.astype(BF16))]
    convert_element_type x1, other arithmetic: 2.39 us -> 4.58 us  [on_device(): final_table = (final_table * (1.0 / math.sqrt(32768))).astype(BF16)]
  transfers between devices with their start and end apart: 1 -> 1, of which waited for: 1 -> 1; matrix products, arithmetic and copies ran while one was open for 23% -> 8% of each run, Pallas kernels for 0% -> 0%
where the time goes in v5:
time: 126 us
  blocking collectives  58.3 us (46%)
  waiting for transfers between devices  23.1 us (18%)
  starting transfers between devices  20.4 us (16%)
  Pallas kernels  13.7 us (11%)
  other arithmetic  7.91 us (6%)
  matrix products  2.5 us (2%)
    all_to_all x1, blocking collectives, on_device(): lax.all_to_all(section_two.reshape(512, 2, 2, 128), EVERYWHERE, 0, 0, til...  48.6 us
    all_to_all x1, waiting for transfers between devices, on_device(): lax.all_to_all(outgoing.reshape(128, 9, 2, 128), ROWS, 0, 0, tiled=True)  23.1 us
    all_to_all x1, starting transfers between devices, on_device(): lax.all_to_all(outgoing.reshape(128, 9, 2, 128), ROWS, 0, 0, tiled=True)  20.4 us
    all_to_all x1, blocking collectives, on_device(): cells = lax.all_to_all(sent, 'cols', 0, 0, tiled=True)  9.71 us
    pallas_call x1, Pallas kernels, on_device(): pl.pallas_call(scatter_body, in_specs=[VMEM] * 2, out_specs=VMEM, out_sha...  5.11 us
    convert_element_type x1, other arithmetic, on_device(): final_table = (final_table * (1.0 / math.sqrt(32768))).astype(BF16)  4.58 us
    pallas_call x1, Pallas kernels, on_device(): pl.pallas_call(final_body, in_specs=[VMEM, VMEM, pl.BlockSpec(memory_spac...  3.51 us
    pallas_call x1, Pallas kernels, on_device(): pl.pallas_call(pack_body, in_specs=[VMEM] * 3, out_specs=VMEM, out_shape=...  3.02 us
  transfers between devices with their start and end apart: 1, of which 1 were waited for; matrix products, arithmetic and copies ran while one was open for 8% of the time, Pallas kernels for 0%

profile of v5, /device:TPU:1, one launch (start us, length us, event | category | flops | bytes accessed | tf_op | source)
XLA Modules:
  0.0 126.1 jit_solution(10560487034872256377)
XLA Ops:
  0.0 3.0 %shard_map.46 = bf16[2304,128]{1,0:T(8,128)(2,1)} custom-call(bf16[64,64,64]{2,1,0:T(8,128)(2,1)} %tiles_ref.1, s32[1,64]{1,0:T(1,128)} %bitcast.10, s32[1,64]{1,0:T(1,128)} %bitcast.11), custom_call_target="tpu_custom_call" | custom-call | tf_op jit(solution)/shard_map/pallas_call | solution.py:214
  3.0 20.4 %all-to-all-start = ((bf16[128,9,2,128]{3,2,1,0:T(2,128)(2,1)}), bf16[128,9,2,128]{3,2,1,0:T(2,128)(2,1)S(1)}, u32[]{:S(2)}, u32[]{:S(2)}) async-start(bf16[128,9,2,128]{3,2,1,0:T(2,128)(2,1)} %bitcast.8), calls=%async_computation | async-start | bytes 1179648 | tf_op jit(solution)/shard_map/all_to_all | solution.py:221
  23.6 0.3 fusion.27.phase_ref
  23.8 0.6 fusion.23.slab_table_ref
  24.4 2.3 %fusion.15.mix_table_ref = bf16[256,512]{1,0:T(8,128)(2,1)S(1)} fusion(s32[512]{0:T(512)S(1)} %broadcast_multiply_fusion, s32[512]{0:T(512)S(1)} %get-tuple-element.20, s32[256]{0:T(256)S(1)} %get-tuple-element.22, s32[512]{0:T(512)S(1)} %get-tuple-element.19, s32[256]{0:T(256)S(1)} %get-tuple-element.21), kind=kLoop, calls=%fused_computation.22 | loop fusion | flops 2490368 | bytes 270336 | tf_op jit(solution)/shard_map/convert_element_type | solution.py:189
  26.7 0.1 fusion.8.order_ref
  26.8 4.6 %fusion.7.table_ref = bf16[512,512]{1,0:T(8,128)(2,1)S(1)} fusion(s32[512]{0:T(512)S(1)} %get-tuple-element.28, s32[512]{0:T(512)S(1)} %get-tuple-element.30, s32[512]{0:T(512)S(1)} %get-tuple-element.29, s32[512]{0:T(512)S(1)} %get-tuple-element.27), kind=kLoop, calls=%fused_computation.10 | loop fusion | flops 4980736 | bytes 532480 | tf_op jit(solution)/shard_map/convert_element_type | solution.py:202
  31.4 2.5 %compare_select_fusion.cell_table_hbm = bf16[1024,1024]{1,0:T(8,128)(2,1)} fusion(s32[1024]{0:T(1024)S(1)} %get-tuple-element.32, s32[1024]{0:T(1024)S(1)} %get-tuple-element.33, s32[1024]{0:T(1024)S(1)} %get-tuple-element.31, s32[1024]{0:T(1024)S(1)} %get-tuple-element.34, s32[128]{0:T(128)S(1)} %get-tuple-element.35, s32[128]{0:T(128)S(1)} %get-tuple-element.36, ...), kind=kOutput, calls=%fused_computation | convolution fusion | flops 304660480 | bytes 2115584 | tf_op jit(solution)/shard_map/dot_general | solution.py:211
  33.9 0.0 copy-start
  33.9 23.1 %all-to-all-done = bf16[128,9,2,128]{3,2,1,0:T(2,128)(2,1)S(1)} async-done(((bf16[128,9,2,128]{3,2,1,0:T(2,128)(2,1)}), bf16[128,9,2,128]{3,2,1,0:T(2,128)(2,1)S(1)}, u32[]{:S(2)}, u32[]{:S(2)}) %all-to-all-start) | async-done | bytes 589856 | tf_op jit(solution)/shard_map/all_to_all | solution.py:221
  57.0 5.1 %shard_map.47 = bf16[4,256,128]{2,1,0:T(8,128)(2,1)} custom-call(bf16[2304,128]{1,0:T(8,128)(2,1)S(1)} %bitcast.6, bf16[512,512]{1,0:T(8,128)(2,1)S(1)} %fusion.8.order_ref), custom_call_target="tpu_custom_call" | custom-call | tf_op jit(solution)/shard_map/pallas_call | solution.py:227
  62.2 9.7 %all_to_all.15.cells_ref = bf16[4,256,128]{2,1,0:T(8,128)(2,1)S(1)} all-to-all(bf16[4,256,128]{2,1,0:T(8,128)(2,1)} %shard_map.47), channel_id=1, replica_groups=mesh['chip'=64,'core'=2,'cols'=4] {'cols'}, dimensions={0} | all-to-all | bytes 524288 | tf_op jit(solution)/shard_map/all_to_all | solution.py:239
  71.9 2.0 %shard_map.48 = bf16[2048,128]{1,0:T(8,128)(2,1)} custom-call(bf16[4,256,128]{2,1,0:T(8,128)(2,1)S(1)} %all_to_all.15.cells_ref, bf16[256,512]{1,0:T(8,128)(2,1)S(1)} %fusion.15.mix_table_ref, bf16[256,128]{1,0:T(8,128)(2,1)S(1)} %fusion.23.slab_table_ref, f32[128,8]{1,0:T(8,128)S(1)} %fusion.27.phase_ref), custom_call_target="tpu_custom_call" | custom-call | tf_op jit(solution)/shard_map/pallas_call | solution.py:240
  73.9 48.6 %all_to_all.16 = bf16[512,2,2,128]{3,2,1,0:T(2,128)(2,1)S(1)} all-to-all(bf16[512,2,2,128]{3,2,1,0:T(2,128)(2,1)} %bitcast.9), channel_id=1, replica_groups=mesh['chip'=64,'core'=2,'cols'=4] {'chip','core','cols'}, dimensions={0} | all-to-all | bytes 1048576 | tf_op jit(solution)/shard_map/all_to_all | solution.py:248
  122.5 0.0 copy-done
  122.5 3.5 %shard_map.49 = f32[256,2,512]{2,1,0:T(2,128)} custom-call(bf16[2048,128]{1,0:T(8,128)(2,1)S(1)} %bitcast.7, bf16[512,512]{1,0:T(8,128)(2,1)S(1)} %fusion.7.table_ref, bf16[1024,1024]{1,0:T(8,128)(2,1)} %compare_select_fusion.cell_table_hbm, bf16[256,512]{1,0:T(8,128)(2,1)S(1)} %copy-done), custom_call_target="tpu_custom_call" | custom-call | tf_op jit(solution)/shard_map/pallas_call | solution.py:251
  (12 shorter events, 0.1 us)
Async XLA Ops:
  3.0 54.0 %all-to-all-start = ((bf16[128,9,2,128]{3,2,1,0:T(2,128)(2,1)}), bf16[128,9,2,128]{3,2,1,0:T(2,128)(2,1)S(1)}, u32[]{:S(2)}, u32[]{:S(2)}) async-start(bf16[128,9,2,128]{3,2,1,0:T(2,128)(2,1)} %bitcast.8), calls=%async_computation | async-start | bytes 1179648 | tf_op jit(solution)/shard_map/all_to_all | solution.py:221
  33.9 88.5 %copy-start = (bf16[256,512]{1,0:T(8,128)(2,1)S(1)}, bf16[256,512]{1,0:T(8,128)(2,1)}, u32[]{:S(2)}) copy-start(bf16[256,512]{1,0:T(8,128)(2,1)} %psf_ref.1) | copy-start | bytes 786436

commit v6 on v5

--- a/solution.py
+++ b/solution.py
@@ -49,7 +49,7 @@
     out_ref[...] = packed_ref[...].astype(BF16)
 
 
-def scatter_body(tiles_ref, order_ref, out_ref, flat_ref, spread_ref, hot_ref):
+def scatter_body(tiles_ref, out_ref, flat_ref, spread_ref, hot_ref):
     flat_ref[...] = tiles_ref[...].astype(F32)
     labels = flat_ref[pl.ds(16, 128, stride=18), :]
     named = jnp.transpose(labels)
@@ -77,9 +77,13 @@
             hot_ref[slot, :, 128 * g : 128 * g + 128] = jnp.where(hot, 1.0, 0.0).astype(BF16)
         part = jnp.dot(hot_ref[slot], spread_ref[slot], preferred_element_type=F32)
         total = part if total is None else total + part
-    total = jnp.dot(total.astype(BF16), order_ref[...], preferred_element_type=F32)
+    total = total.astype(BF16)
+    lane = lax.broadcasted_iota(jnp.int32, (512, 128), 1)
+    source = lane // 8 * 32 + lane % 8
+    given = lax.broadcasted_iota(jnp.int32, (512, 128), 0)
     for octet in range(4):
-        out_ref[octet] = total[:, 128 * octet : 128 * octet + 128].astype(BF16)
+        order = jnp.where(given == source + 8 * octet, 1.0, 0.0).astype(BF16)
+        out_ref[octet] = jnp.dot(total, order, preferred_element_type=F32).astype(BF16)
 
 
 def lane_sign(shape):
@@ -121,25 +125,21 @@
 def final_body(
     rows_ref,
     table_ref,
-    cell_table_hbm,
+    cell_table_ref,
     psf_ref,
     out_ref,
     flat_ref,
     values_ref,
-    cell_table_ref,
     stacked_ref,
     result_ref,
     sems,
 ):
-    fetch = pltpu.make_async_copy(cell_table_hbm, cell_table_ref, sems.at[4])
-    fetch.start()
     flat_ref[...] = rows_ref[...].astype(F32)
     for h in range(8):
         for r in range(4):
             values_ref[64 * r : 64 * r + 64, 128 * h : 128 * h + 128] = flat_ref[
                 pl.ds(4 * h + r, 64, stride=32), :
             ].astype(BF16)
-    fetch.wait()
     spectrum = jnp.dot(values_ref[...], cell_table_ref[...], preferred_element_type=F32)
     stacked_ref[:256] = spectrum[:, :512].astype(BF16)
     stacked_ref[256:] = spectrum[:, 512:].astype(BF16)
@@ -162,6 +162,7 @@
 
 
 VMEM = pl.BlockSpec(memory_space=pltpu.VMEM)
+GRANT = pltpu.CompilerParams(vmem_limit_bytes=16 * 2**20)
 
 
 def in_vmem(x):
@@ -175,10 +176,6 @@
     iota = lambda n: jnp.arange(n, dtype=jnp.int32)
 
     member = 4 * core + me_col
-
-    out = iota(512)
-    source = out % 128 // 8 * 32 + out // 128 * 8 + out % 8
-    order_table = (iota(512)[:, None] == source[None, :]).astype(BF16)
 
     given, out = iota(256)[:, None], iota(512)[None, :]
     column = given // 8 * 64 + 8 * member + given % 8
@@ -219,22 +216,23 @@
         scratch_shapes=[pltpu.VMEM((2048, 128), F32), pltpu.VMEM((2304, 128), F32)],
     )(tile_density, tile_dest.reshape(1, 64), tile_place.reshape(1, 64))
     arrived = lax.all_to_all(outgoing.reshape(128, 9, 2, 128), ROWS, 0, 0, tiled=True)
-    arrived, order_table, mix_table, slab_table, phase, final_table, cell_table = (
+    arrived, mix_table, slab_table, phase, final_table, cell_table = (
         lax.optimization_barrier(
-            (arrived, order_table, mix_table, slab_table, phase, final_table, cell_table)
+            (arrived, mix_table, slab_table, phase, final_table, cell_table)
         )
     )
     sent = pl.pallas_call(
         scatter_body,
-        in_specs=[VMEM] * 2,
+        in_specs=[VMEM],
         out_specs=VMEM,
         out_shape=jax.ShapeDtypeStruct((4, 256, 128), BF16),
+        compiler_params=GRANT,
         scratch_shapes=[
             pltpu.VMEM((2304, 128), F32),
             pltpu.VMEM((2, 512, 512), BF16),
             pltpu.VMEM((2, 256, 512), BF16),
         ],
-    )(in_vmem(arrived.reshape(2304, 128)), in_vmem(order_table))
+    )(in_vmem(arrived.reshape(2304, 128)))
 
     cells = lax.all_to_all(sent, "cols", 0, 0, tiled=True)
     section_two = pl.pallas_call(
@@ -242,6 +240,7 @@
         in_specs=[VMEM] * 4,
         out_specs=VMEM,
         out_shape=jax.ShapeDtypeStruct((2048, 128), BF16),
+        compiler_params=GRANT,
         scratch_shapes=[pltpu.VMEM((2048, 128), F32)],
     )(in_vmem(cells), in_vmem(mix_table), in_vmem(slab_table), in_vmem(phase))
 
@@ -250,21 +249,21 @@
     )
     return pl.pallas_call(
         final_body,
-        in_specs=[VMEM, VMEM, pl.BlockSpec(memory_space=pl.ANY), VMEM],
+        in_specs=[VMEM] * 4,
         out_specs=pl.BlockSpec(memory_space=pl.ANY),
         out_shape=jax.ShapeDtypeStruct((256, 2, 512), F32),
+        compiler_params=GRANT,
         scratch_shapes=[
             pltpu.VMEM((2048, 128), F32),
             pltpu.VMEM((256, 1024), BF16),
-            pltpu.VMEM((1024, 1024), BF16),
             pltpu.VMEM((512, 512), BF16),
             pltpu.VMEM((256, 2, 512), F32),
-            pltpu.SemaphoreType.DMA((5,)),
+            pltpu.SemaphoreType.DMA((4,)),
         ],
     )(
         in_vmem(section_two.reshape(2048, 128)),
         in_vmem(final_table),
-        cell_table,
+        in_vmem(cell_table),
         in_vmem(psf_spectrum),
     )
 

time: 126 us -> 124 us (0.984)
  Pallas kernels: 13.7 us -> 11.2 us
  other arithmetic: 7.91 us -> 9.52 us
    pallas_call x2, Pallas kernels: 8.62 us -> 6.95 us  [the longest x1 4.5 us: on_device(): pl.pallas_call(scatter_body, in_specs=[VMEM], out_specs=VMEM, out_shape=j...]
  transfers between devices with their start and end apart: 1 -> 1, of which waited for: 1 -> 1; matrix products, arithmetic and copies ran while one was open for 8% -> 9% of each run, Pallas kernels for 0% -> 0%
where the time goes in v6:
time: 124 us
  blocking collectives  57.9 us (47%)
  waiting for transfers between devices  22.2 us (18%)
  starting transfers between devices  20.4 us (16%)
  Pallas kernels  11.2 us (9%)
  other arithmetic  9.52 us (8%)
  matrix products  1.85 us (1%)
    all_to_all x1, blocking collectives, on_device(): lax.all_to_all(section_two.reshape(512, 2, 2, 128), EVERYWHERE, 0, 0, til...  48.3 us
    all_to_all x1, waiting for transfers between devices, on_device(): lax.all_to_all(outgoing.reshape(128, 9, 2, 128), ROWS, 0, 0, tiled=True)  22.2 us
    all_to_all x1, starting transfers between devices, on_device(): lax.all_to_all(outgoing.reshape(128, 9, 2, 128), ROWS, 0, 0, tiled=True)  20.4 us
    all_to_all x1, blocking collectives, on_device(): cells = lax.all_to_all(sent, 'cols', 0, 0, tiled=True)  9.52 us
    convert_element_type x1, other arithmetic, on_device(): final_table = (final_table * (1.0 / math.sqrt(32768))).astype(BF16)  4.58 us
    pallas_call x1, Pallas kernels, on_device(): pl.pallas_call(scatter_body, in_specs=[VMEM], out_specs=VMEM, out_shape=j...  4.5 us
    pallas_call x1, Pallas kernels, on_device(): pl.pallas_call(pack_body, in_specs=[VMEM] * 3, out_specs=VMEM, out_shape=...  3.02 us
  transfers between devices with their start and end apart: 1, of which 1 were waited for; matrix products, arithmetic and copies ran while one was open for 9% of the time, Pallas kernels for 0%

profile of v6, /device:TPU:1, one launch (start us, length us, event | category | flops | bytes accessed | tf_op | source)
XLA Modules:
  0.0 124.1 jit_solution(10003225094857893535)
XLA Ops:
  0.0 3.0 %shard_map.46 = bf16[2304,128]{1,0:T(8,128)(2,1)} custom-call(bf16[64,64,64]{2,1,0:T(8,128)(2,1)} %tiles_ref.1, s32[1,64]{1,0:T(1,128)} %bitcast.10, s32[1,64]{1,0:T(1,128)} %bitcast.11), custom_call_target="tpu_custom_call" | custom-call | tf_op jit(solution)/shard_map/pallas_call | solution.py:211
  3.0 20.4 %all-to-all-start = ((bf16[128,9,2,128]{3,2,1,0:T(2,128)(2,1)}), bf16[128,9,2,128]{3,2,1,0:T(2,128)(2,1)S(1)}, u32[]{:S(2)}, u32[]{:S(2)}) async-start(bf16[128,9,2,128]{3,2,1,0:T(2,128)(2,1)} %bitcast.9), calls=%async_computation | async-start | bytes 1179648 | tf_op jit(solution)/shard_map/all_to_all | solution.py:218
  23.4 0.6 and_select_fusion.3
  24.0 0.6 and_select_fusion
  24.7 0.3 fusion.26.phase_ref
  25.0 1.2 fusion.22.slab_table_ref
  26.2 2.2 %fusion.14.mix_table_ref = bf16[256,512]{1,0:T(8,128)(2,1)S(1)} fusion(s32[512]{0:T(512)S(1)} %broadcast_multiply_fusion, s32[512]{0:T(512)S(1)} %get-tuple-element.18, s32[256]{0:T(256)S(1)} %get-tuple-element.20, s32[512]{0:T(512)S(1)} %get-tuple-element.17, s32[256]{0:T(256)S(1)} %get-tuple-element.19), kind=kLoop, calls=%fused_computation.20 | loop fusion | flops 2490368 | bytes 270336 | tf_op jit(solution)/shard_map/convert_element_type | solution.py:186
  28.4 4.6 %fusion.7.table_ref = bf16[512,512]{1,0:T(8,128)(2,1)S(1)} fusion(s32[512]{0:T(512)S(1)} %get-tuple-element.26, s32[512]{0:T(512)S(1)} %get-tuple-element.28, s32[512]{0:T(512)S(1)} %get-tuple-element.27, s32[512]{0:T(512)S(1)} %get-tuple-element.25), kind=kLoop, calls=%fused_computation.10 | loop fusion | flops 4980736 | bytes 532480 | tf_op jit(solution)/shard_map/convert_element_type | solution.py:199
  33.0 1.8 %compare_select_fusion.cell_table_ref = bf16[1024,1024]{1,0:T(8,128)(2,1)S(1)} fusion(s32[1024]{0:T(1024)S(1)} %get-tuple-element.30, s32[1024]{0:T(1024)S(1)} %get-tuple-element.31, s32[1024]{0:T(1024)S(1)} %get-tuple-element.29, s32[1024]{0:T(1024)S(1)} %get-tuple-element.32, s32[128]{0:T(128)} %get-tuple-element.33, s32[128]{0:T(128)} %get-tuple-element.34, ...), kind=kOutput, calls=%fused_computation | convolution fusion | flops 304660480 | bytes 2115584 | tf_op jit(solution)/shard_map/dot_general | solution.py:208
  34.9 22.2 %all-to-all-done = bf16[128,9,2,128]{3,2,1,0:T(2,128)(2,1)S(1)} async-done(((bf16[128,9,2,128]{3,2,1,0:T(2,128)(2,1)}), bf16[128,9,2,128]{3,2,1,0:T(2,128)(2,1)S(1)}, u32[]{:S(2)}, u32[]{:S(2)}) %all-to-all-start) | async-done | bytes 589856 | tf_op jit(solution)/shard_map/all_to_all | solution.py:218
  57.0 0.0 copy-start
  57.1 4.5 %shard_map.47 = bf16[4,256,128]{2,1,0:T(8,128)(2,1)S(1)} custom-call(bf16[2304,128]{1,0:T(8,128)(2,1)S(1)} %bitcast.6), custom_call_target="tpu_custom_call" | custom-call | tf_op jit(solution)/shard_map/pallas_call | solution.py:224
  61.6 9.5 %all_to_all.15.cells_ref = bf16[4,256,128]{2,1,0:T(8,128)(2,1)S(1)} all-to-all(bf16[4,256,128]{2,1,0:T(8,128)(2,1)S(1)} %shard_map.47), channel_id=1, replica_groups=mesh['chip'=64,'core'=2,'cols'=4] {'cols'}, dimensions={0} | all-to-all | bytes 524288 | tf_op jit(solution)/shard_map/all_to_all | solution.py:237
  71.1 0.0 copy-start.1
  71.1 0.8 copy-done.1
  71.9 1.2 shard_map.48
  73.2 48.3 %all_to_all.16 = bf16[512,2,2,128]{3,2,1,0:T(2,128)(2,1)S(1)} all-to-all(bf16[512,2,2,128]{3,2,1,0:T(2,128)(2,1)S(1)} %bitcast.8), channel_id=1, replica_groups=mesh['chip'=64,'core'=2,'cols'=4] {'chip','core','cols'}, dimensions={0} | all-to-all | bytes 1048576 | tf_op jit(solution)/shard_map/all_to_all | solution.py:247
  121.5 0.0 copy-done
  121.5 2.4 %shard_map.49 = f32[256,2,512]{2,1,0:T(2,128)} custom-call(bf16[2048,128]{1,0:T(8,128)(2,1)S(1)} %bitcast.7, bf16[512,512]{1,0:T(8,128)(2,1)S(1)} %fusion.7.table_ref, bf16[1024,1024]{1,0:T(8,128)(2,1)S(1)} %compare_select_fusion.cell_table_ref, bf16[256,512]{1,0:T(8,128)(2,1)S(1)} %copy-done), custom_call_target="tpu_custom_call" | custom-call | tf_op jit(solution)/shard_map/pallas_call | solution.py:250
  (9 shorter events, 0.1 us)
Async XLA Ops:
  3.0 54.0 %all-to-all-start = ((bf16[128,9,2,128]{3,2,1,0:T(2,128)(2,1)}), bf16[128,9,2,128]{3,2,1,0:T(2,128)(2,1)S(1)}, u32[]{:S(2)}, u32[]{:S(2)}) async-start(bf16[128,9,2,128]{3,2,1,0:T(2,128)(2,1)} %bitcast.9), calls=%async_computation | async-start | bytes 1179648 | tf_op jit(solution)/shard_map/all_to_all | solution.py:218
  57.0 64.4 %copy-start = (bf16[256,512]{1,0:T(8,128)(2,1)S(1)}, bf16[256,512]{1,0:T(8,128)(2,1)}, u32[]{:S(2)}) copy-start(bf16[256,512]{1,0:T(8,128)(2,1)} %psf_ref.1) | copy-start | bytes 786436
  71.1 0.8 copy-start.1

commit v7 on v6

--- a/solution.py
+++ b/solution.py
@@ -91,7 +91,11 @@
     return jnp.where(lane < 64, 1.0, -1.0)
 
 
-def rows_body(cells_ref, mix_table_ref, slab_table_ref, phase_ref, out_ref, flat_ref):
+def rows_body(
+    cells_ref, mix_table_ref, slab_table_hbm, phase_ref, out_ref, flat_ref, slab_table_ref, sem
+):
+    fetch = pltpu.make_async_copy(slab_table_hbm, slab_table_ref, sem)
+    fetch.start()
     sign = lane_sign((128, 128))
     left = lax.broadcasted_iota(jnp.int32, (256, 128), 1) < 64
     for low in range(2):
@@ -106,6 +110,8 @@
         spectrum = jnp.dot(
             jnp.concatenate(pairs, 1), mix_table_ref[...], preferred_element_type=F32
         ).astype(BF16)
+        if low == 0:
+            fetch.wait()
         for half in range(2):
             r = 2 * half + low
             values = spectrum[128 * half : 128 * half + 128]
@@ -237,12 +243,21 @@
     cells = lax.all_to_all(sent, "cols", 0, 0, tiled=True)
     section_two = pl.pallas_call(
         rows_body,
-        in_specs=[VMEM] * 4,
+        in_specs=[VMEM, VMEM, pl.BlockSpec(memory_space=pltpu.HBM), VMEM],
         out_specs=VMEM,
         out_shape=jax.ShapeDtypeStruct((2048, 128), BF16),
         compiler_params=GRANT,
-        scratch_shapes=[pltpu.VMEM((2048, 128), F32)],
-    )(in_vmem(cells), in_vmem(mix_table), in_vmem(slab_table), in_vmem(phase))
+        scratch_shapes=[
+            pltpu.VMEM((2048, 128), F32),
+            pltpu.VMEM((256, 128), BF16),
+            pltpu.SemaphoreType.DMA(()),
+        ],
+    )(
+        in_vmem(cells),
+        in_vmem(mix_table),
+        pltpu.with_memory_space_constraint(slab_table, pltpu.HBM),
+        in_vmem(phase),
+    )
 
     section_two = lax.all_to_all(
         section_two.reshape(512, 2, 2, 128), EVERYWHERE, 0, 0, tiled=True

time: 124 us -> 124 us (level)
  no operation moved by 1% of the time
where the time goes in v7:
time: 124 us
  blocking collectives  57.8 us (47%)
  waiting for transfers between devices  22.2 us (18%)
  starting transfers between devices  20.4 us (16%)
  Pallas kernels  11.8 us (10%)
  other arithmetic  9.48 us (8%)
  matrix products  1.85 us (1%)
    all_to_all x1, blocking collectives, on_device(): lax.all_to_all(section_two.reshape(512, 2, 2, 128), EVERYWHERE, 0, 0, til...  48.3 us
    all_to_all x1, waiting for transfers between devices, on_device(): lax.all_to_all(outgoing.reshape(128, 9, 2, 128), ROWS, 0, 0, tiled=True)  22.2 us
    all_to_all x1, starting transfers between devices, on_device(): lax.all_to_all(outgoing.reshape(128, 9, 2, 128), ROWS, 0, 0, tiled=True)  20.4 us
    all_to_all x1, blocking collectives, on_device(): cells = lax.all_to_all(sent, 'cols', 0, 0, tiled=True)  9.52 us
    convert_element_type x1, other arithmetic, on_device(): final_table = (final_table * (1.0 / math.sqrt(32768))).astype(BF16)  4.58 us
    pallas_call x1, Pallas kernels, on_device(): pl.pallas_call(scatter_body, in_specs=[VMEM], out_specs=VMEM, out_shape=j...  4.5 us
    pallas_call x1, Pallas kernels, on_device(): pl.pallas_call(pack_body, in_specs=[VMEM] * 3, out_specs=VMEM, out_shape=...  3.02 us
  transfers between devices with their start and end apart: 1, of which 1 were waited for; matrix products, arithmetic and copies ran while one was open for 9% of the time, Pallas kernels for 0%

profile of v7, /device:TPU:1, one launch (start us, length us, event | category | flops | bytes accessed | tf_op | source)
XLA Modules:
  0.0 123.9 jit_solution(7028939678024286725)
XLA Ops:
  0.0 3.0 %shard_map.46 = bf16[2304,128]{1,0:T(8,128)(2,1)} custom-call(bf16[64,64,64]{2,1,0:T(8,128)(2,1)} %tiles_ref.1, s32[1,64]{1,0:T(1,128)} %bitcast.10, s32[1,64]{1,0:T(1,128)} %bitcast.11), custom_call_target="tpu_custom_call" | custom-call | tf_op jit(solution)/shard_map/pallas_call | solution.py:217
  3.0 20.4 %all-to-all-start = ((bf16[128,9,2,128]{3,2,1,0:T(2,128)(2,1)}), bf16[128,9,2,128]{3,2,1,0:T(2,128)(2,1)S(1)}, u32[]{:S(2)}, u32[]{:S(2)}) async-start(bf16[128,9,2,128]{3,2,1,0:T(2,128)(2,1)} %bitcast.9), calls=%async_computation | async-start | bytes 1179648 | tf_op jit(solution)/shard_map/all_to_all | solution.py:224
  23.4 0.6 and_select_fusion.3
  24.0 0.5 and_select_fusion
  24.7 0.3 fusion.26.phase_ref
  24.9 1.2 fusion.22.slab_table_hbm
  26.1 2.2 %fusion.14.mix_table_ref = bf16[256,512]{1,0:T(8,128)(2,1)S(1)} fusion(s32[512]{0:T(512)S(1)} %broadcast_multiply_fusion, s32[512]{0:T(512)S(1)} %get-tuple-element.18, s32[256]{0:T(256)S(1)} %get-tuple-element.20, s32[512]{0:T(512)S(1)} %get-tuple-element.17, s32[256]{0:T(256)S(1)} %get-tuple-element.19), kind=kLoop, calls=%fused_computation.20 | loop fusion | flops 2490368 | bytes 270336 | tf_op jit(solution)/shard_map/convert_element_type | solution.py:192
  28.4 4.6 %fusion.7.table_ref = bf16[512,512]{1,0:T(8,128)(2,1)S(1)} fusion(s32[512]{0:T(512)S(1)} %get-tuple-element.26, s32[512]{0:T(512)S(1)} %get-tuple-element.28, s32[512]{0:T(512)S(1)} %get-tuple-element.27, s32[512]{0:T(512)S(1)} %get-tuple-element.25), kind=kLoop, calls=%fused_computation.10 | loop fusion | flops 4980736 | bytes 532480 | tf_op jit(solution)/shard_map/convert_element_type | solution.py:205
  33.0 1.9 %compare_select_fusion.cell_table_ref = bf16[1024,1024]{1,0:T(8,128)(2,1)S(1)} fusion(s32[1024]{0:T(1024)S(1)} %get-tuple-element.30, s32[1024]{0:T(1024)S(1)} %get-tuple-element.31, s32[1024]{0:T(1024)S(1)} %get-tuple-element.29, s32[1024]{0:T(1024)S(1)} %get-tuple-element.32, s32[128]{0:T(128)} %get-tuple-element.33, s32[128]{0:T(128)} %get-tuple-element.34, ...), kind=kOutput, calls=%fused_computation | convolution fusion | flops 304660480 | bytes 2115584 | tf_op jit(solution)/shard_map/dot_general | solution.py:214
  34.8 22.2 %all-to-all-done = bf16[128,9,2,128]{3,2,1,0:T(2,128)(2,1)S(1)} async-done(((bf16[128,9,2,128]{3,2,1,0:T(2,128)(2,1)}), bf16[128,9,2,128]{3,2,1,0:T(2,128)(2,1)S(1)}, u32[]{:S(2)}, u32[]{:S(2)}) %all-to-all-start) | async-done | bytes 589856 | tf_op jit(solution)/shard_map/all_to_all | solution.py:224
  57.0 0.0 copy-start
  57.1 4.5 %shard_map.47 = bf16[4,256,128]{2,1,0:T(8,128)(2,1)S(1)} custom-call(bf16[2304,128]{1,0:T(8,128)(2,1)S(1)} %bitcast.6), custom_call_target="tpu_custom_call" | custom-call | tf_op jit(solution)/shard_map/pallas_call | solution.py:230
  61.6 9.5 %all_to_all.15.cells_ref = bf16[4,256,128]{2,1,0:T(8,128)(2,1)S(1)} all-to-all(bf16[4,256,128]{2,1,0:T(8,128)(2,1)S(1)} %shard_map.47), channel_id=1, replica_groups=mesh['chip'=64,'core'=2,'cols'=4] {'cols'}, dimensions={0} | all-to-all | bytes 524288 | tf_op jit(solution)/shard_map/all_to_all | solution.py:243
  71.1 1.9 %shard_map.48 = bf16[2048,128]{1,0:T(8,128)(2,1)S(1)} custom-call(bf16[4,256,128]{2,1,0:T(8,128)(2,1)S(1)} %all_to_all.15.cells_ref, bf16[256,512]{1,0:T(8,128)(2,1)S(1)} %fusion.14.mix_table_ref, bf16[256,128]{1,0:T(8,128)(2,1)} %fusion.22.slab_table_hbm, f32[128,8]{1,0:T(8,128)S(1)} %fusion.26.phase_ref), custom_call_target="tpu_custom_call" | custom-call | tf_op jit(solution)/shard_map/pallas_call | solution.py:244
  72.9 48.3 %all_to_all.16 = bf16[512,2,2,128]{3,2,1,0:T(2,128)(2,1)S(1)} all-to-all(bf16[512,2,2,128]{3,2,1,0:T(2,128)(2,1)S(1)} %bitcast.8), channel_id=1, replica_groups=mesh['chip'=64,'core'=2,'cols'=4] {'chip','core','cols'}, dimensions={0} | all-to-all | bytes 1048576 | tf_op jit(solution)/shard_map/all_to_all | solution.py:262
  121.3 0.0 copy-done
  121.3 2.5 %shard_map.49 = f32[256,2,512]{2,1,0:T(2,128)} custom-call(bf16[2048,128]{1,0:T(8,128)(2,1)S(1)} %bitcast.7, bf16[512,512]{1,0:T(8,128)(2,1)S(1)} %fusion.7.table_ref, bf16[1024,1024]{1,0:T(8,128)(2,1)S(1)} %compare_select_fusion.cell_table_ref, bf16[256,512]{1,0:T(8,128)(2,1)S(1)} %copy-done), custom_call_target="tpu_custom_call" | custom-call | tf_op jit(solution)/shard_map/pallas_call | solution.py:265
  (9 shorter events, 0.1 us)
Async XLA Ops:
  3.0 54.0 %all-to-all-start = ((bf16[128,9,2,128]{3,2,1,0:T(2,128)(2,1)}), bf16[128,9,2,128]{3,2,1,0:T(2,128)(2,1)S(1)}, u32[]{:S(2)}, u32[]{:S(2)}) async-start(bf16[128,9,2,128]{3,2,1,0:T(2,128)(2,1)} %bitcast.9), calls=%async_computation | async-start | bytes 1179648 | tf_op jit(solution)/shard_map/all_to_all | solution.py:224
  57.0 64.2 %copy-start = (bf16[256,512]{1,0:T(8,128)(2,1)S(1)}, bf16[256,512]{1,0:T(8,128)(2,1)}, u32[]{:S(2)}) copy-start(bf16[256,512]{1,0:T(8,128)(2,1)} %psf_ref.1) | copy-start | bytes 786436

commit v8 on v7

--- a/solution.py
+++ b/solution.py
@@ -91,10 +91,8 @@
     return jnp.where(lane < 64, 1.0, -1.0)
 
 
-def rows_body(
-    cells_ref, mix_table_ref, slab_table_hbm, phase_ref, out_ref, flat_ref, slab_table_ref, sem
-):
-    fetch = pltpu.make_async_copy(slab_table_hbm, slab_table_ref, sem)
+def rows_body(cells_ref, tables_ref, phase_hbm, out_ref, flat_ref, phase_ref, sem):
+    fetch = pltpu.make_async_copy(phase_hbm, phase_ref, sem)
     fetch.start()
     sign = lane_sign((128, 128))
     left = lax.broadcasted_iota(jnp.int32, (256, 128), 1) < 64
@@ -108,15 +106,15 @@
                 first = pltpu.roll(first, 64, 1)
             pairs.append(jnp.where(left, first, second).astype(BF16))
         spectrum = jnp.dot(
-            jnp.concatenate(pairs, 1), mix_table_ref[...], preferred_element_type=F32
+            jnp.concatenate(pairs, 1), tables_ref[:, :512], preferred_element_type=F32
         ).astype(BF16)
-        if low == 0:
-            fetch.wait()
         for half in range(2):
             r = 2 * half + low
             values = spectrum[128 * half : 128 * half + 128]
-            both = jnp.dot(slab_table_ref[...], values, preferred_element_type=F32)
+            both = jnp.dot(tables_ref[:, 512:], values, preferred_element_type=F32)
             first, second = both[:128], both[128:]
+            if r == 0:
+                fetch.wait()
             cosine, sine = phase_ref[:, r : r + 1], phase_ref[:, 4 + r : 5 + r]
             straight = first * cosine - second * sine
             crossed = second * cosine + first * sine
@@ -193,6 +191,7 @@
 
     given, out = iota(128)[None, :], iota(256)[:, None]
     slab_table = cosines(given * (out % 128) + 96 * (out // 128), 128).astype(BF16)
+    tables = jnp.concatenate([mix_table, slab_table], 1)
     part = iota(8)[None, :]
     phase = cosines(
         (64 * (part % 4) + chip) * iota(128)[:, None] + 24576 * (part // 4), 32768
@@ -222,10 +221,8 @@
         scratch_shapes=[pltpu.VMEM((2048, 128), F32), pltpu.VMEM((2304, 128), F32)],
     )(tile_density, tile_dest.reshape(1, 64), tile_place.reshape(1, 64))
     arrived = lax.all_to_all(outgoing.reshape(128, 9, 2, 128), ROWS, 0, 0, tiled=True)
-    arrived, mix_table, slab_table, phase, final_table, cell_table = (
-        lax.optimization_barrier(
-            (arrived, mix_table, slab_table, phase, final_table, cell_table)
-        )
+    arrived, tables, phase, final_table, cell_table = lax.optimization_barrier(
+        (arrived, tables, phase, final_table, cell_table)
     )
     sent = pl.pallas_call(
         scatter_body,
@@ -243,20 +240,19 @@
     cells = lax.all_to_all(sent, "cols", 0, 0, tiled=True)
     section_two = pl.pallas_call(
         rows_body,
-        in_specs=[VMEM, VMEM, pl.BlockSpec(memory_space=pltpu.HBM), VMEM],
+        in_specs=[VMEM, VMEM, pl.BlockSpec(memory_space=pltpu.HBM)],
         out_specs=VMEM,
         out_shape=jax.ShapeDtypeStruct((2048, 128), BF16),
         compiler_params=GRANT,
         scratch_shapes=[
             pltpu.VMEM((2048, 128), F32),
-            pltpu.VMEM((256, 128), BF16),
+            pltpu.VMEM((128, 8), F32),
             pltpu.SemaphoreType.DMA(()),
         ],
     )(
         in_vmem(cells),
-        in_vmem(mix_table),
-        pltpu.with_memory_space_constraint(slab_table, pltpu.HBM),
-        in_vmem(phase),
+        in_vmem(tables),
+        pltpu.with_memory_space_constraint(phase, pltpu.HBM),
     )
 
     section_two = lax.all_to_all(

time: 124 us -> 124 us (level)
  no operation moved by 1% of the time
where the time goes in v8:
time: 124 us
  blocking collectives  57.9 us (47%)
  waiting for transfers between devices  22.2 us (18%)
  starting transfers between devices  20.4 us (16%)
  Pallas kernels  12 us (10%)
  other arithmetic  9.52 us (8%)
  matrix products  1.86 us (2%)
    all_to_all x1, blocking collectives, on_device(): lax.all_to_all(section_two.reshape(512, 2, 2, 128), EVERYWHERE, 0, 0, til...  48.4 us
    all_to_all x1, waiting for transfers between devices, on_device(): lax.all_to_all(outgoing.reshape(128, 9, 2, 128), ROWS, 0, 0, tiled=True)  22.2 us
    all_to_all x1, starting transfers between devices, on_device(): lax.all_to_all(outgoing.reshape(128, 9, 2, 128), ROWS, 0, 0, tiled=True)  20.4 us
    all_to_all x1, blocking collectives, on_device(): cells = lax.all_to_all(sent, 'cols', 0, 0, tiled=True)  9.52 us
    convert_element_type x1, other arithmetic, on_device(): final_table = (final_table * (1.0 / math.sqrt(32768))).astype(BF16)  4.55 us
    pallas_call x1, Pallas kernels, on_device(): pl.pallas_call(scatter_body, in_specs=[VMEM], out_specs=VMEM, out_shape=j...  4.5 us
    pallas_call x1, Pallas kernels, on_device(): pl.pallas_call(pack_body, in_specs=[VMEM] * 3, out_specs=VMEM, out_shape=...  3.02 us
  transfers between devices with their start and end apart: 1, of which 1 were waited for; matrix products, arithmetic and copies ran while one was open for 9% of the time, Pallas kernels for 0%

profile of v8, /device:TPU:1, one launch (start us, length us, event | category | flops | bytes accessed | tf_op | source)
XLA Modules:
  0.0 124.0 jit_solution(17692018796771537347)
XLA Ops:
  0.0 3.0 %shard_map.46 = bf16[2304,128]{1,0:T(8,128)(2,1)} custom-call(bf16[64,64,64]{2,1,0:T(8,128)(2,1)} %tiles_ref.1, s32[1,64]{1,0:T(1,128)} %bitcast.10, s32[1,64]{1,0:T(1,128)} %bitcast.11), custom_call_target="tpu_custom_call" | custom-call | tf_op jit(solution)/shard_map/pallas_call | solution.py:216
  3.0 20.4 %all-to-all-start = ((bf16[128,9,2,128]{3,2,1,0:T(2,128)(2,1)}), bf16[128,9,2,128]{3,2,1,0:T(2,128)(2,1)S(1)}, u32[]{:S(2)}, u32[]{:S(2)}) async-start(bf16[128,9,2,128]{3,2,1,0:T(2,128)(2,1)} %bitcast.9), calls=%async_computation | async-start | bytes 1179648 | tf_op jit(solution)/shard_map/all_to_all | solution.py:223
  23.4 0.6 and_select_fusion.3
  24.0 0.5 and_select_fusion
  24.7 0.6 fusion.22
  25.2 2.2 %fusion.14 = bf16[256,512]{1,0:T(8,128)(2,1)S(1)} fusion(s32[512]{0:T(512)S(1)} %broadcast_multiply_fusion, s32[512]{0:T(512)S(1)} %get-tuple-element.18, s32[256]{0:T(256)S(1)} %get-tuple-element.20, s32[512]{0:T(512)S(1)} %get-tuple-element.17, s32[256]{0:T(256)S(1)} %get-tuple-element.19), kind=kLoop, calls=%fused_computation.20 | loop fusion | flops 2490368 | bytes 270336 | tf_op jit(solution)/shard_map/convert_element_type | solution.py:190
  27.5 0.9 fusion.26.phase_hbm
  28.4 4.6 %fusion.7.table_ref = bf16[512,512]{1,0:T(8,128)(2,1)S(1)} fusion(s32[512]{0:T(512)S(1)} %get-tuple-element.24, s32[512]{0:T(512)S(1)} %get-tuple-element.26, s32[512]{0:T(512)S(1)} %get-tuple-element.25, s32[512]{0:T(512)S(1)} %get-tuple-element.23), kind=kLoop, calls=%fused_computation.10 | loop fusion | flops 4980736 | bytes 532480 | tf_op jit(solution)/shard_map/convert_element_type | solution.py:204
  33.0 1.9 %compare_select_fusion.cell_table_ref = bf16[1024,1024]{1,0:T(8,128)(2,1)S(1)} fusion(s32[1024]{0:T(1024)S(1)} %get-tuple-element.28, s32[1024]{0:T(1024)S(1)} %get-tuple-element.29, s32[1024]{0:T(1024)S(1)} %get-tuple-element.27, s32[1024]{0:T(1024)S(1)} %get-tuple-element.30, s32[128]{0:T(128)} %get-tuple-element.31, s32[128]{0:T(128)} %get-tuple-element.32, ...), kind=kOutput, calls=%fused_computation | convolution fusion | flops 304660480 | bytes 2115584 | tf_op jit(solution)/shard_map/dot_general | solution.py:213
  34.9 22.2 %all-to-all-done = bf16[128,9,2,128]{3,2,1,0:T(2,128)(2,1)S(1)} async-done(((bf16[128,9,2,128]{3,2,1,0:T(2,128)(2,1)}), bf16[128,9,2,128]{3,2,1,0:T(2,128)(2,1)S(1)}, u32[]{:S(2)}, u32[]{:S(2)}) %all-to-all-start) | async-done | bytes 589856 | tf_op jit(solution)/shard_map/all_to_all | solution.py:223
  57.0 0.0 copy-start
  57.1 4.5 %shard_map.47 = bf16[4,256,128]{2,1,0:T(8,128)(2,1)S(1)} custom-call(bf16[2304,128]{1,0:T(8,128)(2,1)S(1)} %bitcast.6), custom_call_target="tpu_custom_call" | custom-call | tf_op jit(solution)/shard_map/pallas_call | solution.py:227
  61.6 9.5 %all_to_all.15.cells_ref = bf16[4,256,128]{2,1,0:T(8,128)(2,1)S(1)} all-to-all(bf16[4,256,128]{2,1,0:T(8,128)(2,1)S(1)} %shard_map.47), channel_id=1, replica_groups=mesh['chip'=64,'core'=2,'cols'=4] {'cols'}, dimensions={0} | all-to-all | bytes 524288 | tf_op jit(solution)/shard_map/all_to_all | solution.py:240
  71.1 2.0 %shard_map.48 = bf16[2048,128]{1,0:T(8,128)(2,1)S(1)} custom-call(bf16[4,256,128]{2,1,0:T(8,128)(2,1)S(1)} %all_to_all.15.cells_ref, bf16[256,640]{1,0:T(8,128)(2,1)S(1)} %pad_maximum_fusion.tables_ref, f32[128,8]{1,0:T(8,128)} %fusion.26.phase_hbm), custom_call_target="tpu_custom_call" | custom-call | tf_op jit(solution)/shard_map/pallas_call | solution.py:241
  73.1 48.4 %all_to_all.16 = bf16[512,2,2,128]{3,2,1,0:T(2,128)(2,1)S(1)} all-to-all(bf16[512,2,2,128]{3,2,1,0:T(2,128)(2,1)S(1)} %bitcast.8), channel_id=1, replica_groups=mesh['chip'=64,'core'=2,'cols'=4] {'chip','core','cols'}, dimensions={0} | all-to-all | bytes 1048576 | tf_op jit(solution)/shard_map/all_to_all | solution.py:258
  121.4 0.0 copy-done
  121.4 2.5 %shard_map.49 = f32[256,2,512]{2,1,0:T(2,128)} custom-call(bf16[2048,128]{1,0:T(8,128)(2,1)S(1)} %bitcast.7, bf16[512,512]{1,0:T(8,128)(2,1)S(1)} %fusion.7.table_ref, bf16[1024,1024]{1,0:T(8,128)(2,1)S(1)} %compare_select_fusion.cell_table_ref, bf16[256,512]{1,0:T(8,128)(2,1)S(1)} %copy-done), custom_call_target="tpu_custom_call" | custom-call | tf_op jit(solution)/shard_map/pallas_call | solution.py:261
  (10 shorter events, 0.1 us)
Async XLA Ops:
  3.0 54.0 %all-to-all-start = ((bf16[128,9,2,128]{3,2,1,0:T(2,128)(2,1)}), bf16[128,9,2,128]{3,2,1,0:T(2,128)(2,1)S(1)}, u32[]{:S(2)}, u32[]{:S(2)}) async-start(bf16[128,9,2,128]{3,2,1,0:T(2,128)(2,1)} %bitcast.9), calls=%async_computation | async-start | bytes 1179648 | tf_op jit(solution)/shard_map/all_to_all | solution.py:223
  57.0 64.4 %copy-start = (bf16[256,512]{1,0:T(8,128)(2,1)S(1)}, bf16[256,512]{1,0:T(8,128)(2,1)}, u32[]{:S(2)}) copy-start(bf16[256,512]{1,0:T(8,128)(2,1)} %psf_ref.1) | copy-start | bytes 786436
